TPU v7x, 128 devices: a whole 4x4x4 slice. The times are simulated.
128 devices in a mesh: row: 16 (over y, z_lo, core), col: 8 (over z_hi, x).
Axes of the slice: x: 4, y: 4, z: 4 (z_hi: 2, z_lo: 2; z = z_hi * 2 + z_lo), core: 2. Of those that a mesh axis runs over, the one named last changes fastest.
Arguments:
- z_trunk: bfloat16 [1024, 1024, 128], P('row', 'col'), may hold values from -6 to 6
- coords: int32 [3, 1024], P(None, ('row', 'col')), may hold values from 0 to 255
- token_mask: int32 [1024], P(('row', 'col')), may hold values 0 or 1
- w_dist: bfloat16 [39, 128], replicated, may hold values from -6 to 6
- w_attn: bfloat16 [128, 512], replicated, may hold values from -0.5 to 0.5
- w_bias: bfloat16 [128, 4], replicated, may hold values from -100 to 100
- w_out: bfloat16 [128, 128], replicated, may hold values from -2 to 2
- w_pae: bfloat16 [128, 64], replicated, may hold values from -0.5 to 0.5
- w_pde: bfloat16 [128, 64], replicated, may hold values from -0.5 to 0.5
Outputs:
- logits: float32 [1024, 1024, 128], P('row', 'col')
All inputs are finite; a program needn't handle non-finite values. No bound on the sum of `token_mask` on one device may be relied on, other than what follows from the above.
Results may differ from a plain program's by a relative error of at most 0.0055.
The roundings to bfloat16 on the way count: a program that leaves them out, or rounds other values in their place, can miss the bound.
Values may be sent and summed in bfloat16 or wider, within the bound.
A program may use at most 192 MiB of HBM per device.

v0:
```python
import jax
import jax.numpy as jnp
from jax import lax
from jax.sharding import PartitionSpec as P


def layer_norm(values):
    widened = values.astype(jnp.float32)
    average = jnp.mean(widened, axis=-1, keepdims=True)
    centred = widened - average
    variance = jnp.mean(centred * centred, axis=-1, keepdims=True)
    return (centred * lax.rsqrt(variance + 1e-05)).astype(jnp.bfloat16)


def distance_bins(coord_rows, coord_cols, class_count):
    offsets = coord_rows[:, :, None] - coord_cols[:, None, :]
    squared = jnp.sum(offsets * offsets, axis=0)
    bin_edges = 27 + 4 * jnp.arange(class_count - 1, dtype=jnp.int32)
    above = (squared[:, :, None] > (bin_edges * bin_edges)[None, None, :]).astype(jnp.int32)
    return jnp.sum(above, axis=-1)


def attend_column(query_rows, key_rows, value_rows, bias_full, key_bias):
    length_all = query_rows.shape[0]
    block_rows = min(512, length_all)

    def one_block(first_row):
        query_block = lax.dynamic_slice_in_dim(query_rows, first_row, block_rows, 0)
        bias_block = lax.dynamic_slice_in_dim(bias_full, first_row, block_rows, 2)
        scores = jnp.einsum(
            "khd,ihd->hki", key_rows, query_block, preferred_element_type=jnp.float32
        )
        scores = scores + bias_block + key_bias[None, :, None]
        highest = jnp.max(scores, axis=1, keepdims=True)
        raised = jnp.exp(scores - highest)
        weights = (raised / jnp.sum(raised, axis=1, keepdims=True)).astype(jnp.bfloat16)
        return jnp.einsum("hki,khd->ihd", weights, value_rows, preferred_element_type=jnp.float32)

    starts = jnp.arange(length_all // block_rows, dtype=jnp.int32) * block_rows
    blocks_out = lax.map(one_block, starts)
    return blocks_out.reshape(length_all, query_rows.shape[1], query_rows.shape[2])


def error_logits(updated, mirrored, w_pae, w_pde):
    width = updated.shape[-1]
    symmetric = updated.astype(jnp.float32) + mirrored.astype(jnp.float32)
    pae_part = jnp.dot(
        layer_norm(updated).reshape(-1, width), w_pae, preferred_element_type=jnp.float32
    )
    pde_part = jnp.dot(
        layer_norm(symmetric).reshape(-1, width), w_pde, preferred_element_type=jnp.float32
    )
    return jnp.concatenate([pae_part, pde_part], axis=1).reshape(
        updated.shape[0], updated.shape[1], -1
    )


def per_device(z_trunk, coords, token_mask, w_dist, w_attn, w_bias, w_out, w_pae, w_pde):
    all_coords, all_mask = (
        lax.all_gather(coords, ("row", "col"), axis=1, tiled=True),
        lax.all_gather(token_mask, ("row", "col"), axis=0, tiled=True),
    )
    rows_dev = z_trunk.shape[0]
    cols_dev = z_trunk.shape[1]
    width = z_trunk.shape[2]
    n_rows = lax.axis_size("row")
    n_cols = lax.axis_size("col")
    total = rows_dev * n_rows
    slab = rows_dev // n_cols
    heads = w_bias.shape[1]
    head_dim = width // heads
    classes = w_dist.shape[0]
    row_first = lax.axis_index("row") * rows_dev
    col_first = lax.axis_index("col") * cols_dev
    coord_rows = lax.dynamic_slice_in_dim(all_coords, row_first, rows_dev, 1)
    coord_cols = lax.dynamic_slice_in_dim(all_coords, col_first, cols_dev, 1)
    bins_tile = distance_bins(coord_rows, coord_cols, classes)
    one_hot = (bins_tile[:, :, None] == jnp.arange(classes, dtype=jnp.int32)[None, None, :]).astype(
        jnp.bfloat16
    )
    embedded = jnp.dot(one_hot.reshape(-1, classes), w_dist, preferred_element_type=jnp.float32)
    pair = (z_trunk.astype(jnp.float32) + embedded.reshape(rows_dev, cols_dev, width)).astype(
        jnp.bfloat16
    )
    pair_cols = lax.all_to_all(pair, "row", split_axis=1, concat_axis=0, tiled=True)
    normed = layer_norm(pair_cols)
    flat_normed = normed.reshape(-1, width)
    projected = jnp.dot(flat_normed, w_attn, preferred_element_type=jnp.float32)
    query_all = (
        (projected[:, :width] * head_dim ** (-0.5))
        .astype(jnp.bfloat16)
        .reshape(total, slab, heads, head_dim)
    )
    key_all = (
        projected[:, width : 2 * width].astype(jnp.bfloat16).reshape(total, slab, heads, head_dim)
    )
    value_all = (
        projected[:, 2 * width : 3 * width]
        .astype(jnp.bfloat16)
        .reshape(total, slab, heads, head_dim)
    )
    gate_all = projected[:, 3 * width :].astype(jnp.bfloat16)
    bias_local = jnp.einsum("kic,ch->hki", normed, w_bias, preferred_element_type=jnp.float32)
    gathered = lax.all_gather(bias_local, ("row", "col"), axis=2, tiled=True)
    bias_full = (
        gathered.reshape(heads, total, n_rows, n_cols, slab)
        .transpose(0, 1, 3, 2, 4)
        .reshape(heads, total, total)
    )
    key_bias = (all_mask.astype(jnp.float32) - 1.0) * 30000.0

    def one_column(operands):
        query_rows, key_rows, value_rows = operands
        return attend_column(query_rows, key_rows, value_rows, bias_full, key_bias)

    attended = lax.map(
        one_column,
        (jnp.swapaxes(query_all, 0, 1), jnp.swapaxes(key_all, 0, 1), jnp.swapaxes(value_all, 0, 1)),
    )
    attended = jnp.swapaxes(attended, 0, 1).reshape(total * slab, width)
    gated = (jax.nn.sigmoid(gate_all.astype(jnp.float32)) * attended).astype(jnp.bfloat16)
    update = jnp.dot(gated, w_out, preferred_element_type=jnp.float32)
    updated = (pair_cols.reshape(-1, width).astype(jnp.float32) + update).astype(jnp.bfloat16)
    updated = updated.reshape(total, slab, width)
    pieces = updated.reshape(n_cols, n_rows, slab, slab, width).transpose(1, 0, 2, 3, 4)
    flat_pieces = pieces.reshape(n_rows * n_cols, slab, slab, width)
    moved = lax.all_to_all(flat_pieces, ("row", "col"), split_axis=0, concat_axis=0, tiled=True)
    moved = moved.reshape(n_rows, n_cols, slab, slab, width)
    mirrored = moved.transpose(1, 0, 3, 2, 4).reshape(total, slab, width)
    logits_cols = error_logits(updated, mirrored, w_pae, w_pde)
    return lax.all_to_all(
        logits_cols.astype(jnp.bfloat16), "row", split_axis=0, concat_axis=1, tiled=True
    ).astype(logits_cols.dtype)


def solution(mesh):
    in_specs = (
        P("row", "col", None),
        P(None, ("row", "col")),
        P(("row", "col")),
        P(),
        P(),
        P(),
        P(),
        P(),
        P(),
    )
    out_specs = P("row", "col", None)
    return jax.shard_map(
        per_device, mesh=mesh, in_specs=in_specs, out_specs=out_specs, check_vma=False
    )
```

profile of v0, /device:TPU:31, one launch (start us, length us, event | category | flops | bytes accessed | tf_op | source)
XLA Modules:
  0.0 1153.4 jit_solution(17012444799415025751)
XLA Ops:
  6.5 271.7 %all-gather = s32[128,8,3]{1,2,0:T(4,128)S(1)} all-gather(s32[1,8,3]{1,2,0:T(4,128)} %bitcast.145), channel_id=1, replica_groups=mesh['row'=16,'col'=8] {'row','col'}, dimensions={0}, use_global_device_ids=true | all-gather | bytes 12384 | tf_op jit(solution)/shard_map/all_gather | solution.py:60
  283.0 64.7 %all_to_all.23 = bf16[64,128,128]{2,0,1:T(8,128)(2,1)S(1)} all-to-all(bf16[64,128,128]{2,0,1:T(8,128)(2,1)S(1)} %copy.130), channel_id=1, replica_groups=mesh['row'=16,'col'=8] {'row'}, dimensions={1} | all-to-all | bytes 4194304 | tf_op jit(solution)/shard_map/all_to_all | solution.py:85
  350.5 6.8 multiply_reduce_fusion.1
  365.8 9.3 convolution_bitcast_fusion
  376.8 73.8 %all-reduce = s32[1024]{0:T(1024)S(1)} all-reduce(s32[1024]{0:T(1024)S(1)} %dynamic-update-slice), channel_id=1, replica_groups=mesh['row'=16,'col'=8] {'row','col'}, use_global_device_ids=true, to_apply=%add | all-reduce | flops 1024 | bytes 8192
  451.1 6.1 fusion.30
  457.3 8.0 fusion.48
  469.1 11.7 %reshape.172 = bf16[1024,8,4,32]{3,2,1,0:T(4,128)(2,1)} reshape(bf16[8192,128]{1,0:T(8,128)(2,1)} %get-tuple-element.162) | data formatting | bytes 4194304 | tf_op jit(solution)/shard_map/reshape | solution.py:95
  480.9 12.2 %copy.146 = bf16[8,1024,4,32]{1,3,2,0:T(8,128)(2,1)} copy(bf16[8,1024,4,32]{3,2,0,1:T(4,128)(2,1)} %bitcast.133) | data formatting | bytes 4194304 | tf_op jit(solution)/shard_map/while | solution.py:116
  493.1 6.1 reshape.173
  499.2 12.2 %copy.147 = bf16[8,1024,4,32]{1,3,2,0:T(8,128)(2,1)} copy(bf16[8,1024,4,32]{3,2,0,1:T(4,128)(2,1)} %bitcast.134) | data formatting | bytes 4194304 | tf_op jit(solution)/shard_map/while | solution.py:116
  513.9 6.1 reshape.171
  520.0 12.2 %copy.145 = bf16[8,1024,4,32]{1,3,2,0:T(8,128)(2,1)} copy(bf16[8,1024,4,32]{3,2,0,1:T(4,128)(2,1)} %bitcast.135) | data formatting | bytes 4194304 | tf_op jit(solution)/shard_map/while | solution.py:116
  532.2 174.9 %all-gather.3.cloned.1.call-done = f32[4,1024,1024]{1,0,2:T(4,128)} async-done(((f32[4,1024,8]{1,0,2:T(4,128)}), f32[4,1024,1024]{1,0,2:T(4,128)}) %all-gather.3.cloned.1.call-update) | async-done | bytes 16777232 | tf_op jit(solution)/shard_map/all_gather | solution.py:104
  707.1 17.7 %copy.144 = f32[4,1024,8,16,8]{1,4,3,2,0:T(8,128)} copy(f32[4,1024,8,16,8]{1,0,4,2,3:T(4,128)} %bitcast.138) | data formatting | bytes 33554432 | tf_op jit(solution)/shard_map/transpose | solution.py:107
  724.8 297.9 %while.21 = (s32[]{:T(128)}, f32[8,1024,4,32]{3,2,1,0:T(4,128)}, bf16[8,1024,4,32]{1,3,2,0:T(8,128)(2,1)}, bf16[8,1024,4,32]{1,3,2,0:T(8,128)(2,1)}, bf16[8,1024...) while((s32[]{:T(128)}, f32[8,1024,4,32]{3,2,1,0:T(4,128)}, ...), condition=%wide.region_9.10_spmd, body=%wide.region_4.9_spmd.sunk | while | flops 421531648 | bytes 23358848 | solution.py:116
  727.3 32.8 %while.22 = (s32[]{:T(128)}, f32[2,512,4,32]{1,3,2,0:T(8,128)S(1)}, s32[2]{0:T(128)S(1)}, bf16[1024,4,32]{0,2,1:T(8,128)(2,1)S(1)}, bf16[1024,4,32]{0,2,1:T(8,12...) while((s32[]{:T(128)}, f32[2,512,4,32]{1,3,2,0:T(8,128)S(1)}, ...), condition=%wide.region_8.8_spmd, body=%wide.region_5.7_spmd.sunk | while | flops 421531648 | bytes 18115228 | solution.py:40
  729.9 5.7 fusion.70
  735.6 8.2 fusion.71
  751.9 8.1 fusion.71
  764.5 32.8 %while.22 = (s32[]{:T(128)}, f32[2,512,4,32]{1,3,2,0:T(8,128)S(1)}, s32[2]{0:T(128)S(1)}, bf16[1024,4,32]{0,2,1:T(8,128)(2,1)S(1)}, bf16[1024,4,32]{0,2,1:T(8,12...) while((s32[]{:T(128)}, f32[2,512,4,32]{1,3,2,0:T(8,128)S(1)}, ...), condition=%wide.region_8.8_spmd, body=%wide.region_5.7_spmd.sunk | while | flops 421531648 | bytes 18115228 | solution.py:40
  772.8 8.2 fusion.71
  789.1 8.1 fusion.71
  801.7 32.8 %while.22 = (s32[]{:T(128)}, f32[2,512,4,32]{1,3,2,0:T(8,128)S(1)}, s32[2]{0:T(128)S(1)}, bf16[1024,4,32]{0,2,1:T(8,128)(2,1)S(1)}, bf16[1024,4,32]{0,2,1:T(8,12...) while((s32[]{:T(128)}, f32[2,512,4,32]{1,3,2,0:T(8,128)S(1)}, ...), condition=%wide.region_8.8_spmd, body=%wide.region_5.7_spmd.sunk | while | flops 421531648 | bytes 18115228 | solution.py:40
  809.9 8.2 fusion.71
  826.3 8.1 fusion.71
  838.9 32.8 %while.22 = (s32[]{:T(128)}, f32[2,512,4,32]{1,3,2,0:T(8,128)S(1)}, s32[2]{0:T(128)S(1)}, bf16[1024,4,32]{0,2,1:T(8,128)(2,1)S(1)}, bf16[1024,4,32]{0,2,1:T(8,12...) while((s32[]{:T(128)}, f32[2,512,4,32]{1,3,2,0:T(8,128)S(1)}, ...), condition=%wide.region_8.8_spmd, body=%wide.region_5.7_spmd.sunk | while | flops 421531648 | bytes 18115228 | solution.py:40
  847.1 8.2 fusion.71
  863.5 8.1 fusion.71
  876.0 32.8 %while.22 = (s32[]{:T(128)}, f32[2,512,4,32]{1,3,2,0:T(8,128)S(1)}, s32[2]{0:T(128)S(1)}, bf16[1024,4,32]{0,2,1:T(8,128)(2,1)S(1)}, bf16[1024,4,32]{0,2,1:T(8,12...) while((s32[]{:T(128)}, f32[2,512,4,32]{1,3,2,0:T(8,128)S(1)}, ...), condition=%wide.region_8.8_spmd, body=%wide.region_5.7_spmd.sunk | while | flops 421531648 | bytes 18115228 | solution.py:40
  878.6 5.7 fusion.70
  884.3 8.2 fusion.71
  900.7 8.1 fusion.71
  913.3 32.8 %while.22 = (s32[]{:T(128)}, f32[2,512,4,32]{1,3,2,0:T(8,128)S(1)}, s32[2]{0:T(128)S(1)}, bf16[1024,4,32]{0,2,1:T(8,128)(2,1)S(1)}, bf16[1024,4,32]{0,2,1:T(8,12...) while((s32[]{:T(128)}, f32[2,512,4,32]{1,3,2,0:T(8,128)S(1)}, ...), condition=%wide.region_8.8_spmd, body=%wide.region_5.7_spmd.sunk | while | flops 421531648 | bytes 18115228 | solution.py:40
  921.5 8.2 fusion.71
  937.9 8.1 fusion.71
  950.4 32.8 %while.22 = (s32[]{:T(128)}, f32[2,512,4,32]{1,3,2,0:T(8,128)S(1)}, s32[2]{0:T(128)S(1)}, bf16[1024,4,32]{0,2,1:T(8,128)(2,1)S(1)}, bf16[1024,4,32]{0,2,1:T(8,12...) while((s32[]{:T(128)}, f32[2,512,4,32]{1,3,2,0:T(8,128)S(1)}, ...), condition=%wide.region_8.8_spmd, body=%wide.region_5.7_spmd.sunk | while | flops 421531648 | bytes 18115228 | solution.py:40
  958.7 8.2 fusion.71
  975.1 8.1 fusion.71
  987.7 32.8 %while.22 = (s32[]{:T(128)}, f32[2,512,4,32]{1,3,2,0:T(8,128)S(1)}, s32[2]{0:T(128)S(1)}, bf16[1024,4,32]{0,2,1:T(8,128)(2,1)S(1)}, bf16[1024,4,32]{0,2,1:T(8,12...) while((s32[]{:T(128)}, f32[2,512,4,32]{1,3,2,0:T(8,128)S(1)}, ...), condition=%wide.region_8.8_spmd, body=%wide.region_5.7_spmd.sunk | while | flops 421531648 | bytes 18115228 | solution.py:40
  990.2 5.7 fusion.70
  995.9 8.2 fusion.71
  1012.3 8.1 fusion.71
  1022.8 15.3 %copy.148 = f32[1024,8,4,32]{3,2,1,0:T(4,128)} copy(f32[1024,8,4,32]{3,2,0,1:T(4,128)} %bitcast.139) | data formatting | bytes 8388608 | tf_op jit(solution)/shard_map/transpose | solution.py:120
  1038.1 13.5 %reshape.176 = f32[8192,128]{1,0:T(8,128)} reshape(f32[1024,8,4,32]{3,2,1,0:T(4,128)} %copy.148) | data formatting | bytes 8388608 | tf_op jit(solution)/shard_map/reshape | solution.py:120
  1058.7 9.9 all-to-all-start.1
  1068.6 26.5 %all-to-all-done.1 = bf16[128,8,8,128]{3,2,1,0:T(8,128)(2,1)} async-done(((bf16[128,8,8,128]{3,2,1,0:T(8,128)(2,1)}), bf16[128,8,8,128]{3,2,1,0:T(8,128)(2,1)}, u32[]{:S(2)}, u32[]{:S(2)}) %all-to-all-start.1) | async-done | bytes 2097184 | tf_op jit(solution)/shard_map/all_to_all | solution.py:127
  1113.8 30.0 %all_to_all.24 = bf16[1024,8,128]{2,1,0:T(8,128)(2,1)S(1)} all-to-all(bf16[1024,8,128]{2,1,0:T(8,128)(2,1)} %bitcast.142), channel_id=1, replica_groups=mesh['row'=16,'col'=8] {'row'}, dimensions={0} | all-to-all | bytes 4194304 | tf_op jit(solution)/shard_map/all_to_all | solution.py:131
  (140 shorter events, 172.0 us)
Async XLA Ops:
  6.5 450.7 %copy-start = (bf16[128,512]{1,0:T(8,128)(2,1)S(1)}, bf16[128,512]{1,0:T(8,128)(2,1)}, u32[]{:S(2)}) copy-start(bf16[128,512]{1,0:T(8,128)(2,1)} %param.17) | copy-start | bytes 393220
  6.5 700.6 %all-gather.3.cloned.1.call-start = ((), (), s32[]{:S(2)}) async-start(), calls=%async_computation.3 | async-start | bytes 16908288 | tf_op jit(solution)/shard_map/all_gather | solution.py:104
  360.5 2.0 copy-start.2
  360.5 5.3 copy-start.5
  365.8 10.8 copy-start.8
  465.3 3.8 copy-start.3
  1038.1 13.5 %copy-start.6 = (bf16[128,128]{1,0:T(8,128)(2,1)S(1)}, bf16[128,128]{1,0:T(8,128)(2,1)}, u32[]{:S(2)}) copy-start(bf16[128,128]{1,0:T(8,128)(2,1)} %param.19) | copy-start | bytes 98308
  1058.7 36.4 %all-to-all-start.1 = ((bf16[128,8,8,128]{3,2,1,0:T(8,128)(2,1)}), bf16[128,8,8,128]{3,2,1,0:T(8,128)(2,1)}, u32[]{:S(2)}, u32[]{:S(2)}) async-start(bf16[128,8,8,128]{3,2,1,0:T(8,128)(2,1)} %bitcast.141), calls=%async_computation.1 | async-start | bytes 4194304 | tf_op jit(solution)/shard_map/all_to_all | solution.py:127
  1102.0 3.0 copy-start.7
  1102.0 6.1 copy-start.4
  1113.8 32.6 %copy-start.1 = (bf16[128,512]{1,0:T(8,128)(2,1)S(1)}, bf16[128,512]{1,0:T(8,128)(2,1)}, u32[]{:S(2)}) copy-start(bf16[128,512]{1,0:T(8,128)(2,1)} %param.17) | copy-start | bytes 393220
Sparse Core Ops, SparseCore 0:
  376.7 330.4 all-gather.2
where the time goes:
time: 1170 us; the launch traced here: 1150 us
  blocking collectives  440 us (38%)
  matrix products  253 us (22%)
  waiting for transfers between devices  201 us (17%)
  local copies, waits for them, and re-layouts  170 us (15%)
  other arithmetic  33.9 us (3%)
  loops' own time  31.4 us (3%)
  between operations  13.9 us (1%)
    all_gather x1, blocking collectives, per_device(): lax.all_gather(coords, ('row', 'col'), axis=1, tiled=True)  272 us
    all_gather x1, waiting for transfers between devices, per_device(): gathered = lax.all_gather(bias_local, ('row', 'col'), axis=2, tiled=True)  175 us
    dot_general x16, matrix products, one_block(): jnp.einsum('hki,khd->ihd', weights, value_rows, preferred_element_type=jn...  130 us
    sub x16, matrix products, one_block(): raised = jnp.exp(scores - highest)  90.4 us
    unnamed x1, blocking collectives  73.8 us
    all_to_all x1, blocking collectives, per_device(): lax.all_to_all(pair, 'row', split_axis=1, concat_axis=0, tiled=True)  64.7 us
    while x3, local copies, waits for them, and re-layouts, per_device(): lax.map(one_column, (jnp.swapaxes(query_all, 0, 1), jnp.swapaxes(key_all,...  36.7 us
    another operation x8, loops' own time, attend_column(): blocks_out = lax.map(one_block, starts)  30.7 us
  transfers between devices with their start and end apart: 2, of which 2 were waited for; matrix products, arithmetic and copies ran while one was open for 7% of the time, Pallas kernels for 0%

commit v1 on v0

v1 whole, which is shorter than its diff:
```python
import functools

import jax
import jax.numpy as jnp
from jax import lax
from jax.experimental import pallas as pl
from jax.experimental.pallas import tpu as pltpu
from jax.sharding import PartitionSpec as P

MESH = pl.DeviceIdType.MESH
BF = jnp.bfloat16
F32 = jnp.float32
LOG2E = 1.4426950408889634
ORDERS = (("y", "z", "x"), ("z", "x", "y"), ("x", "y", "z"))
ROWS = ((0, 24), (24, 24), (48, 16))


def layer_norm(values):
    widened = values.astype(F32)
    average = jnp.mean(widened, axis=-1, keepdims=True)
    centred = widened - average
    variance = jnp.mean(centred * centred, axis=-1, keepdims=True)
    return (centred * lax.rsqrt(variance + 1e-05)).astype(BF)


def remote(src, dst, send, recv, device):
    return pltpu.make_async_remote_copy(
        src_ref=src, dst_ref=dst, send_sem=send, recv_sem=recv, device_id=device, device_id_type=MESH
    )


def embed_kernel(z_ref, sub_ref, lane_ref, wd_ref, wb_ref, pair_ref, bias_ref,
                 rs, rl, flat, s_send, s_recv, l_send, l_recv):
    row = lax.axis_index("row")
    col = lax.axis_index("col")
    slot = lax.rem(row, 2) * 8 + col
    target = row // 2
    barrier = pltpu.get_barrier_semaphore()

    def greet_row(d, _):
        pl.semaphore_signal(barrier, inc=1, device_id=(row, lax.rem(col + d, 8)), device_id_type=MESH)
        return 0

    lax.fori_loop(1, 8, greet_row, 0)

    def greet_source(s, _):
        src_row = 2 * col + s // 8
        src_col = lax.rem(s, 8)

        @pl.when(jnp.logical_or(src_row != row, src_col != col))
        def _():
            pl.semaphore_signal(barrier, inc=1, device_id=(src_row, src_col), device_id_type=MESH)

        return 0

    lax.fori_loop(0, 16, greet_source, 0)

    @pl.when(target == col)
    def _():
        pl.semaphore_wait(barrier, 22)

    @pl.when(target != col)
    def _():
        pl.semaphore_wait(barrier, 23)

    def row_copy(d):
        to = lax.rem(col + d, 8)
        return remote(sub_ref, rs.at[col], s_send.at[d - 1], s_recv.at[d - 1], (row, to))

    def lane_copy(r):
        return remote(lane_ref, rl.at[slot], l_send.at[r], l_recv.at[slot], (r, target))

    def lane_arrival(s):
        return remote(lane_ref, rl.at[s], l_send.at[s], l_recv.at[s], (2 * col + s // 8, lax.rem(s, 8)))

    def start_row(d, _):
        row_copy(d).start()
        return 0

    lax.fori_loop(1, 8, start_row, 0)

    def start_lane(r, _):
        @pl.when(jnp.logical_or(r != row, target != col))
        def _():
            lane_copy(r).start()

        return 0

    lax.fori_loop(0, 16, start_lane, 0)
    rs[col] = sub_ref[...]

    @pl.when(target == col)
    def _():
        rl[slot] = lane_ref[...]

    def wait_row(d, _):
        row_copy(d).wait()
        return 0

    lax.fori_loop(1, 8, wait_row, 0)

    def wait_lane(r, _):
        @pl.when(jnp.logical_or(r != row, target != col))
        def _():
            lane_copy(r).wait_send()

        @pl.when(jnp.logical_or(2 * col + r // 8 != row, lax.rem(r, 8) != col))
        def _():
            lane_arrival(r).wait_recv()

        return 0

    lax.fori_loop(0, 16, wait_lane, 0)

    lanes = jnp.sum(rl[...], axis=0)
    cx, cy, cz = lanes[0:1], lanes[1:2], lanes[2:3]
    edge = lax.broadcasted_iota(jnp.int32, (40, 128), 0)
    upper_edge = 27 + 4 * edge
    lower_edge = 23 + 4 * edge
    big = jnp.int32(1 << 20)
    lower = jnp.where(edge == 0, -1, jnp.where(edge == 39, big, lower_edge * lower_edge)).astype(F32)
    upper = jnp.where(edge >= 38, big, upper_edge * upper_edge).astype(F32)
    wd = wd_ref[...]
    wb = wb_ref[...]

    def eight(t, _):
        own = rs[t]
        dx = own[:, 0:1] - cx
        dy = own[:, 1:2] - cy
        dz = own[:, 2:3] - cz
        squared = dx * dx + dy * dy + dz * dz
        key_bias = (own[:, 3:4] - 1.0) * 30000.0
        rows = []
        for a in range(8):
            i = t * 8 + a
            here = jnp.broadcast_to(squared[a : a + 1], (40, 128))
            hot = jnp.where(jnp.logical_and(here > lower, here <= upper), 1.0, 0.0).astype(BF)
            added = lax.dot_general(hot, wd, (((0,), (0,)), ((), ())), preferred_element_type=F32)
            pair = (z_ref[i].astype(F32) + added).astype(BF)
            flat[pl.ds(i, 128, stride=64), :] = pair.astype(F32)
            normed = layer_norm(pair)
            b = lax.dot_general(wb, normed, (((1,), (1,)), ((), ())), preferred_element_type=F32)
            rows.append(b + key_bias[a : a + 1])
        start = pl.multiple_of(t * 8, 8)
        for h in range(4):
            bias_ref[h, pl.ds(start, 8), :] = jnp.concatenate([r[h : h + 1] for r in rows], axis=0)
        return 0

    lax.fori_loop(0, 8, eight, 0)

    def out(g, _):
        for j in range(8):
            at = pl.multiple_of((g * 8 + j) * 64, 64)
            pair_ref[g, j] = flat[pl.ds(at, 64), :].astype(BF)
        return 0

    lax.fori_loop(0, 16, out, 0)


def embed(z, sub, lane, wd, wb):
    return pl.pallas_call(
        embed_kernel,
        out_shape=(
            jax.ShapeDtypeStruct((16, 8, 64, 128), BF),
            jax.ShapeDtypeStruct((4, 64, 128), F32),
        ),
        in_specs=[pl.BlockSpec(memory_space=pltpu.VMEM)] * 5,
        out_specs=(pl.BlockSpec(memory_space=pltpu.VMEM),) * 2,
        scratch_shapes=[
            pltpu.VMEM((8, 8, 128), F32),
            pltpu.VMEM((16, 8, 128), F32),
            pltpu.VMEM((8192, 128), F32),
            pltpu.SemaphoreType.DMA((7,)),
            pltpu.SemaphoreType.DMA((7,)),
            pltpu.SemaphoreType.DMA((16,)),
            pltpu.SemaphoreType.DMA((16,)),
        ],
        compiler_params=pltpu.CompilerParams(collective_id=0, has_side_effects=True, vmem_limit_bytes=40 << 20),
        name="embed",
    )(z, sub, lane, wd, wb)


def place():
    row = lax.axis_index("row")
    col = lax.axis_index("col")
    core = lax.rem(row, 2)
    at = {"x": lax.rem(col, 4), "y": row // 4, "z": (col // 4) * 2 + lax.rem(row // 2, 2)}
    return row, col, core, at


def device_of(at, core):
    return (at["y"] * 4 + lax.rem(at["z"], 2) * 2 + core, (at["z"] // 2) * 4 + at["x"])


def beside(at, dim, delta):
    moved = dict(at)
    moved[dim] = lax.rem(at[dim] + delta + 4, 4)
    return moved


def entry_kernel(pair_ref, bias_ref, out_ref, g0, g1, g2, own_v, send, recv, psend, precv, lsem, asend, arecv, osem):
    row, col, core, at = place()
    gs = (g0, g1, g2)
    partner = device_of(at, 1 - core)
    barrier = pltpu.get_barrier_semaphore()

    def greet(d, _):
        pl.semaphore_signal(barrier, inc=1, device_id=(lax.rem(row + d, 16), col), device_id_type=MESH)
        return 0

    lax.fori_loop(1, 16, greet, 0)
    for dim in ("x", "y", "z"):
        for delta in (1, -1):
            pl.semaphore_signal(barrier, inc=1, device_id=device_of(beside(at, dim, delta), core), device_id_type=MESH)
    pl.semaphore_wait(barrier, 21)

    def a2a(d):
        to = lax.rem(row + d, 16)
        return remote(pair_ref.at[to], out_ref.at[row], asend.at[d - 1], arecv.at[d - 1], (to, col))

    load_own = pltpu.make_async_copy(pair_ref.at[row], own_v, osem.at[0])
    load_own.start()
    pending = []
    partner_waits = []

    def to_partner(p, n, src, dst):
        c = remote(src, dst, psend.at[p, n], precv.at[p, n], partner)
        c.start()
        partner_waits.append(c)

    locals_ = []
    firsts = {}

    def begin(stage, p):
        dims = ORDERS[p]
        a1, a2, a3 = (at[d] for d in dims)
        first, count = ROWS[p]
        g = gs[p]
        if stage == 0:
            src = bias_ref.at[:, pl.ds(first, count), :]
            dst = g.at[core, a3, a2, a1]
            keep = pltpu.make_async_copy(src, dst, lsem.at[p])
            keep.start()
            locals_.append(keep)
            to_partner(p, 0, src, dst)
        elif stage == 1:
            src = dst = g.at[core, a3, a2]
        else:
            src = dst = g.at[core, a3]
        d = dims[stage]
        for k, delta in enumerate((1, -1)):
            c = remote(src, dst, send.at[p, stage * 4 + k], recv.at[p, stage * 4 + k],
                       device_of(beside(at, d, delta), core))
            c.start()
            pending.append(c)
            firsts[stage, p, k] = c

    def block(stage, p, delta):
        dims = ORDERS[p]
        a = [at[d] for d in dims]
        a[stage] = lax.rem(a[stage] + delta + 4, 4)
        a1, a2, a3 = a
        g = gs[p]
        if stage == 0:
            return g.at[core, a3, a2, a1]
        if stage == 1:
            return g.at[core, a3, a2]
        return g.at[core, a3]

    def forward(stage, p):
        d = ORDERS[p][stage]
        for k, delta in enumerate((1, -1)):
            firsts[stage, p, k].wait_recv()
            got = block(stage, p, -delta)
            half = got.at[pl.ds(2 * k, 2)]
            c = remote(half, half, send.at[p, stage * 4 + 2 + k], recv.at[p, stage * 4 + 2 + k],
                       device_of(beside(at, d, delta), core))
            c.start()
            pending.append(c)
            firsts[stage, p, 2 + k] = c
            to_partner(p, 1 + stage * 4 + k, got, got)

    def finish(stage, p):
        for k in (0, 1):
            firsts[stage, p, 2 + k].wait_recv()
            half = block(stage, p, 2).at[pl.ds(2 * k, 2)]
            to_partner(p, 3 + stage * 4 + k, half, half)

    def start_a2a(first, last):
        def go(d, _):
            a2a(d).start()
            return 0

        lax.fori_loop(first, last, go, 0)

    for p in range(3):
        begin(0, p)
    for p in range(3):
        forward(0, p)
    for p in range(3):
        finish(0, p)
    for c in locals_:
        c.wait()
    for p in range(3):
        begin(1, p)
    start_a2a(1, 16)
    load_own.wait()
    save_own = pltpu.make_async_copy(own_v, out_ref.at[row], osem.at[1])
    save_own.start()
    for p in range(3):
        forward(1, p)
    for p in range(3):
        finish(1, p)
    for p in range(3):
        begin(2, p)
    for p in range(3):
        forward(2, p)
    for p in range(3):
        finish(2, p)
    save_own.wait()

    def wait_a2a(d, _):
        a2a(d).wait()
        return 0

    lax.fori_loop(1, 16, wait_a2a, 0)
    for c in partner_waits:
        c.wait()
    for c in pending:
        c.wait_send()


def entry(pair, bias):
    any_spec = pl.BlockSpec(memory_space=pl.ANY)
    return pl.pallas_call(
        entry_kernel,
        out_shape=(jax.ShapeDtypeStruct((16, 8, 64, 128), BF),)
        + tuple(jax.ShapeDtypeStruct((2, 4, 4, 4, 4, n, 128), F32) for _, n in ROWS),
        in_specs=[any_spec, pl.BlockSpec(memory_space=pltpu.VMEM)],
        out_specs=(any_spec,) * 4,
        scratch_shapes=[
            pltpu.VMEM((8, 64, 128), BF),
            pltpu.SemaphoreType.DMA((3, 12)),
            pltpu.SemaphoreType.DMA((3, 12)),
            pltpu.SemaphoreType.DMA((3, 13)),
            pltpu.SemaphoreType.DMA((3, 13)),
            pltpu.SemaphoreType.DMA((3,)),
            pltpu.SemaphoreType.DMA((15,)),
            pltpu.SemaphoreType.DMA((15,)),
            pltpu.SemaphoreType.DMA((2,)),
        ],
        compiler_params=pltpu.CompilerParams(collective_id=1, has_side_effects=True),
        name="entry",
    )(pair, bias)


def attn_kernel(x_ref, b0, b1, b2, wa_ref, wo_ref, o_ref, q_s, k_s, v_s, g_s, s_s, a_s):
    step = pl.program_id(0)

    @pl.when(step == 0)
    def _():
        def one(j, _):
            p = jnp.dot(layer_norm(x_ref[:, j].reshape(1024, 128)), wa_ref[...], preferred_element_type=F32)
            q_s[j] = (p[:, :128] * (32**-0.5)).astype(BF)
            k_s[j] = p[:, 128:256].astype(BF)
            v_s[j] = p[:, 256:384].astype(BF).T
            g_s[j] = p[:, 384:].astype(BF)
            return 0

        lax.fori_loop(0, 8, one, 0)

    head_of_lane = lax.broadcasted_iota(jnp.int32, (256, 128), 1) // 32
    ones = jnp.ones((16, 256), BF)
    i0 = pl.multiple_of(step * 256, 256)
    bs = (b0, b1, b2)

    def bias_piece(kb, h, x):
        parts = []
        for zl in range(2):
            for core in range(2):
                for p in range(3):
                    where = {"x": x, "y": kb, "z": zl}
                    d1, d2, d3 = ORDERS[p]
                    parts.append(bs[p][core, where[d3], where[d2], where[d1], h])
        return jnp.concatenate(parts, axis=0)

    def one(j, _):
        q = q_s[j, pl.ds(i0, 256), :]
        for h in range(4):
            qm = jnp.where(head_of_lane == h, q, jnp.zeros_like(q))
            mx = None
            for kb in range(4):
                s = lax.dot_general(k_s[j, pl.ds(kb * 256, 256), :], qm, (((1,), (1,)), ((), ())),
                                    preferred_element_type=F32)
                s = s + jnp.concatenate([bias_piece(kb, h, 0), bias_piece(kb, h, 1)], axis=1)
                s_s[h % 2, kb] = s
                t = jnp.max(s.reshape(32, 8, 256), axis=0)
                mx = t if mx is None else jnp.maximum(mx, t)
            m = jnp.max(mx, axis=0, keepdims=True)
            acc = None
            for kb in range(4):
                d = (s_s[h % 2, kb] - m) * LOG2E
                p = jnp.exp2(d.astype(BF))
                lhs = jnp.concatenate([v_s[j, h * 32 : h * 32 + 32, kb * 256 : kb * 256 + 256], ones], axis=0)
                r = jnp.dot(lhs, p, preferred_element_type=F32)
                acc = r if acc is None else acc + r
            a_s[h * 32 : h * 32 + 32] = acc[:32] / acc[32:33]
        att = a_s[...].T
        g = g_s[j, pl.ds(i0, 256), :].astype(F32)
        gated = (att / (1.0 + jnp.exp(-g))).astype(BF)
        upd = jnp.dot(gated, wo_ref[...], preferred_element_type=F32)
        x = x_ref[pl.ds(step * 4, 4), j].reshape(256, 128)
        o_ref[j] = (x.astype(F32) + upd).astype(BF)
        return 0

    lax.fori_loop(0, 8, one, 0)


def attend(x, gs, wa, wo):
    def bias_spec(p):
        d1, d2, d3 = ORDERS[p]
        size = {"x": 2, "y": 4, "z": 2}

        def index(c):
            pick = {"x": c % 2, "y": 0, "z": c // 2}
            return (0, pick[d3], pick[d2], pick[d1], 0, 0, 0)

        return pl.BlockSpec((2, size[d3], size[d2], size[d1], 4, ROWS[p][1], 128), index)

    return pl.pallas_call(
        attn_kernel,
        grid=(4,),
        out_shape=jax.ShapeDtypeStruct((8, 1024, 128), BF),
        in_specs=[
            pl.BlockSpec((16, 8, 64, 128), lambda c: (0, 0, 0, 0)),
            bias_spec(0),
            bias_spec(1),
            bias_spec(2),
            pl.BlockSpec((128, 512), lambda c: (0, 0)),
            pl.BlockSpec((128, 128), lambda c: (0, 0)),
        ],
        out_specs=pl.BlockSpec((8, 256, 128), lambda c: (0, c, 0)),
        scratch_shapes=[
            pltpu.VMEM((8, 1024, 128), BF),
            pltpu.VMEM((8, 1024, 128), BF),
            pltpu.VMEM((8, 128, 1024), BF),
            pltpu.VMEM((8, 1024, 128), BF),
            pltpu.VMEM((2, 4, 256, 256), F32),
            pltpu.VMEM((128, 256), F32),
        ],
        compiler_params=pltpu.CompilerParams(vmem_limit_bytes=60 << 20),
        name="attend",
    )(x, *gs, wa, wo)


def exit_kernel(u_ref, d_ref, m_ref, own_d, own_m, dsend, drecv, msend, mrecv, osem):
    row = lax.axis_index("row")
    col = lax.axis_index("col")
    to_row = 2 * col + row // 8
    slot = lax.rem(row, 8)
    src_col = row // 2
    src_row0 = lax.rem(row, 2) * 8
    barrier = pltpu.get_barrier_semaphore()

    def greet(d, _):
        pl.semaphore_signal(barrier, inc=1, device_id=(lax.rem(row + d, 16), col), device_id_type=MESH)
        return 0

    lax.fori_loop(1, 16, greet, 0)
    mine = jnp.logical_and(to_row == row, True)

    def greet_source(s, _):
        @pl.when(jnp.logical_or(src_row0 + s != row, src_col != col))
        def _():
            pl.semaphore_signal(barrier, inc=1, device_id=(src_row0 + s, src_col), device_id_type=MESH)

        return 0

    lax.fori_loop(0, 8, greet_source, 0)

    @pl.when(mine)
    def _():
        pl.semaphore_wait(barrier, 22)

    @pl.when(jnp.logical_not(mine))
    def _():
        pl.semaphore_wait(barrier, 23)

    def direct(d):
        to = lax.rem(row + d, 16)
        return remote(u_ref.at[:, pl.ds(pl.multiple_of(to * 64, 64), 64), :], d_ref.at[row],
                      dsend.at[d - 1], drecv.at[d - 1], (to, col))

    def mirror(c):
        return remote(u_ref.at[:, pl.ds(pl.multiple_of(c * 128, 128), 128), :], m_ref.at[slot],
                      msend.at[c], mrecv.at[slot], (to_row, c))

    def arrival(s):
        return remote(u_ref.at[:, pl.ds(0, 128), :], m_ref.at[s], msend.at[s], mrecv.at[s], (src_row0 + s, src_col))

    def start_mirror(t, _):
        c = lax.rem(col + t, 8)

        @pl.when(jnp.logical_or(to_row != row, c != col))
        def _():
            mirror(c).start()

        return 0

    def start_direct(d, _):
        direct(d).start()
        return 0

    lax.fori_loop(0, 8, start_mirror, 0)
    lax.fori_loop(1, 16, start_direct, 0)
    in_d = pltpu.make_async_copy(u_ref.at[:, pl.ds(pl.multiple_of(row * 64, 64), 64), :], own_d, osem.at[0])
    in_d.start()
    in_d.wait()
    out_d = pltpu.make_async_copy(own_d, d_ref.at[row], osem.at[1])
    out_d.start()

    @pl.when(mine)
    def _():
        in_m = pltpu.make_async_copy(u_ref.at[:, pl.ds(pl.multiple_of(col * 128, 128), 128), :], own_m, osem.at[2])
        in_m.start()
        in_m.wait()
        out_m = pltpu.make_async_copy(own_m, m_ref.at[slot], osem.at[3])
        out_m.start()
        out_m.wait()

    out_d.wait()

    def wait_direct(d, _):
        direct(d).wait()
        return 0

    lax.fori_loop(1, 16, wait_direct, 0)

    def wait_mirror(s, _):
        @pl.when(jnp.logical_or(to_row != row, s != col))
        def _():
            mirror(s).wait_send()

        @pl.when(jnp.logical_or(src_row0 + s != row, src_col != col))
        def _():
            arrival(s).wait_recv()

        return 0

    lax.fori_loop(0, 8, wait_mirror, 0)


def leave(u):
    any_spec = pl.BlockSpec(memory_space=pl.ANY)
    return pl.pallas_call(
        exit_kernel,
        out_shape=(jax.ShapeDtypeStruct((16, 8, 64, 128), BF), jax.ShapeDtypeStruct((8, 8, 128, 128), BF)),
        in_specs=[any_spec],
        out_specs=(any_spec,) * 2,
        scratch_shapes=[
            pltpu.VMEM((8, 64, 128), BF),
            pltpu.VMEM((8, 128, 128), BF),
            pltpu.SemaphoreType.DMA((15,)),
            pltpu.SemaphoreType.DMA((15,)),
            pltpu.SemaphoreType.DMA((8,)),
            pltpu.SemaphoreType.DMA((8,)),
            pltpu.SemaphoreType.DMA((4,)),
        ],
        compiler_params=pltpu.CompilerParams(collective_id=2, has_side_effects=True),
        name="leave",
    )(u)


def logits_kernel(d_ref, m_ref, wp_ref, we_ref, o_ref, flat):
    step = pl.program_id(0)

    @pl.when(step == 0)
    def _():
        def widen(g, _):
            for j in range(8):
                at = pl.multiple_of((g * 8 + j) * 64, 64)
                flat[pl.ds(at, 64), :] = d_ref[g, j].astype(F32)
            return 0

        lax.fori_loop(0, 16, widen, 0)

    for a in range(8):
        u = flat[pl.ds(step * 8 + a, 128, stride=64), :]
        sym = u + m_ref[a].astype(F32)
        pae = jnp.dot(layer_norm(u), wp_ref[...], preferred_element_type=F32)
        pde = jnp.dot(layer_norm(sym), we_ref[...], preferred_element_type=F32)
        o_ref[a] = pae + pde


def logits(d, m, wp, we):
    return pl.pallas_call(
        logits_kernel,
        grid=(8,),
        out_shape=jax.ShapeDtypeStruct((64, 128, 128), F32),
        in_specs=[
            pl.BlockSpec((16, 8, 64, 128), lambda t: (0, 0, 0, 0)),
            pl.BlockSpec((8, 128, 128), lambda t: (t, 0, 0)),
            pl.BlockSpec((128, 128), lambda t: (0, 0)),
            pl.BlockSpec((128, 128), lambda t: (0, 0)),
        ],
        out_specs=pl.BlockSpec((8, 128, 128), lambda t: (t, 0, 0)),
        scratch_shapes=[pltpu.VMEM((8192, 128), F32)],
        compiler_params=pltpu.CompilerParams(vmem_limit_bytes=40 << 20),
        name="logits",
    )(d, m, wp, we)


def per_device(z_trunk, coords, token_mask, w_dist, w_attn, w_bias, w_out, w_pae, w_pde):
    device = lax.axis_index("row") * 8 + lax.axis_index("col")
    info = jnp.concatenate([coords, token_mask[None]], axis=0).astype(F32)
    sub = jnp.pad(info.T, ((0, 0), (0, 124)))
    lane = jnp.arange(128, dtype=jnp.int32)[None, :] // 8 == lax.rem(device, 16)
    lane = jnp.where(lane, jnp.tile(info, (2, 16)), 0.0)
    wd = jnp.pad(w_dist, ((0, 1), (0, 0)))
    wb = jnp.pad(w_bias.T, ((0, 4), (0, 0)))
    pair, bias = embed(z_trunk, sub, lane, wd, wb)
    columns, *gs = entry(pair, bias)
    updated = attend(columns, gs, w_attn, w_out)
    direct, mirror = leave(updated)
    wp = jnp.pad(w_pae, ((0, 0), (0, 64)))
    we = jnp.pad(w_pde, ((0, 0), (64, 0)))
    return logits(direct, mirror.reshape(64, 128, 128), wp, we)


def solution(mesh):
    in_specs = (P("row", "col", None), P(None, ("row", "col")), P(("row", "col")), P(), P(), P(), P(), P(), P())
    return jax.shard_map(
        per_device, mesh=mesh, in_specs=in_specs, out_specs=P("row", "col", None), check_vma=False
    )
```

time: 1170 us -> 320 us (0.27)
  the two profiles are of different devices: /device:TPU:31 before, /device:TPU:97 now
where the time goes in v1:
time: 320 us
  Pallas kernels  310 us (97%)
  local copies, waits for them, and re-layouts  10.2 us (3%)
    pallas_call x1, Pallas kernels, leave(): pl.pallas_call(exit_kernel, out_shape=(jax.ShapeDtypeStruct((16, 8, 64, 1...  112 us
    pallas_call x1, Pallas kernels, attend(): pl.pallas_call(attn_kernel, grid=(4,), out_shape=jax.ShapeDtypeStruct((8,...  82.3 us
    pallas_call x1, Pallas kernels, entry(): pl.pallas_call(entry_kernel, out_shape=(jax.ShapeDtypeStruct((16, 8, 64,...  75.7 us
    pallas_call x1, Pallas kernels, embed(): pl.pallas_call(embed_kernel, out_shape=(jax.ShapeDtypeStruct((16, 8, 64,...  28.1 us
    pallas_call x1, Pallas kernels, logits(): pl.pallas_call(logits_kernel, grid=(8,), out_shape=jax.ShapeDtypeStruct((...  11.3 us
    unnamed x17, local copies, waits for them, and re-layouts  7.73 us

profile of v1, /device:TPU:97, one launch (start us, length us, event | category | flops | bytes accessed | tf_op | source)
XLA Modules:
  0.0 320.1 jit_solution(7578757584384202201)
XLA Ops:
  0.0 0.8 copy.15
  0.8 0.7 copy.16
  1.5 0.1 add_convert_fusion
  1.6 0.1 copy.17
  1.7 0.1 tile.10
  1.8 0.1 fusion.1
  1.9 0.7 pad.21.wd_ref
  2.6 0.7 pad.22.wb_ref
  3.2 0.0 copy-start
  3.3 1.6 copy-done
  4.8 28.1 %embed.1 = (bf16[16,8,64,128]{3,2,1,0:T(8,128)(2,1)S(1)}, f32[4,64,128]{2,1,0:T(8,128)S(1)}) custom-call(bf16[64,128,128]{2,1,0:T(8,128)(2,1)S(1)} %copy-done, f32[8,128]{1,0:T(8,128)S(1)} %pad.20.sub_ref, f32[8,128]{1,0:T(8,128)S(1)} %broadcast_select_fusion.lane_ref, bf16[40,128]{1,0:T(8,128)(2,1)S(1)} %pad.21.wd_ref, bf16[8,128]{1,0:T(8,128)(2,1)S(1)} %pad.22.wb_ref), custom_call_target="tpu_custom_call" | custom-call | tf_op jit(solution)/shard_map/embed/pallas_call | solution.py:161
  32.9 0.0 copy-start.1
  32.9 1.3 copy-done.1
  34.3 0.0 copy-start.4
  34.3 0.7 copy-done.4
  34.9 75.7 %entry.1 = (bf16[16,8,64,128]{3,2,1,0:T(8,128)(2,1)}, f32[2,4,4,4,4,24,128]{6,5,4,3,2,1,0:T(8,128)}, f32[2,4,4,4,4,24,128]{6,5,4,3,2,1,0:T(8,128)}, f32[2,4,4,4,4,16,128]{6,5,4,3,2,1,0:T(8,128)}) custom-call(bf16[16,8,64,128]{3,2,1,0:T(8,128)(2,1)} %copy-done.1, f32[4,64,128]{2,1,0:T(8,128)} %copy-done.4), custom_call_target="tpu_custom_call" | custom-call | tf_op jit(solution)/shard_map/entry/pallas_call | solution.py:335
  110.6 82.3 %attend.1.u_ref = bf16[8,1024,128]{2,1,0:T(8,128)(2,1)} custom-call(bf16[16,8,64,128]{3,2,1,0:T(8,128)(2,1)} %get-tuple-element.15.x_ref, f32[2,4,4,4,4,24,128]{6,5,4,3,2,1,0:T(8,128)} %get-tuple-element.16.b0, f32[2,4,4,4,4,24,128]{6,5,4,3,2,1,0:T(8,128)} %get-tuple-element.17.b1, f32[2,4,4,4,4,16,128]{6,5,4,3,2,1,0:T(8,128)} %get-tuple-element.18.b2, ...), custom_call_target="tpu_custom_call" | custom-call | tf_op jit(solution)/shard_map/attend/pallas_call | solution.py:430
  192.9 0.0 copy-start.5
  192.9 0.0 copy-start.6
  192.9 112.3 %leave.1 = (bf16[16,8,64,128]{3,2,1,0:T(8,128)(2,1)}, bf16[8,8,128,128]{3,2,1,0:T(8,128)(2,1)}) custom-call(bf16[8,1024,128]{2,1,0:T(8,128)(2,1)} %attend.1.u_ref), custom_call_target="tpu_custom_call" | custom-call | tf_op jit(solution)/shard_map/leave/pallas_call | solution.py:555
  305.2 0.0 copy-done.5
  305.2 0.1 copy.18
  305.3 0.0 copy-done.6
  305.3 0.1 copy.19
  305.5 0.1 pad.24.we_ref
  305.5 0.0 copy-start.2
  305.5 1.6 copy-done.2
  307.1 0.0 copy-start.3
  307.1 1.6 copy-done.3
  308.7 11.3 %logits.1 = f32[64,128,128]{2,1,0:T(8,128)} custom-call(bf16[16,8,64,128]{3,2,1,0:T(8,128)(2,1)S(1)} %copy-done.2, bf16[64,128,128]{2,1,0:T(8,128)(2,1)S(1)} %bitcast.7, bf16[128,128]{1,0:T(8,128)(2,1)S(1)} %pad.23.wp_ref, bf16[128,128]{1,0:T(8,128)(2,1)S(1)} %pad.24.we_ref), custom_call_target="tpu_custom_call" | custom-call | tf_op jit(solution)/shard_map/logits/pallas_call | solution.py:596
  (5 shorter events, 0.0 us)
Async XLA Ops:
  3.2 1.6 copy-start
  32.9 1.3 copy-start.1
  34.3 0.7 copy-start.4
  192.9 112.3 %copy-start.5 = (bf16[128,64]{0,1:T(8,128)(2,1)S(1)}, bf16[128,64]{0,1:T(8,128)(2,1)}, u32[]{:S(2)}) copy-start(bf16[128,64]{0,1:T(8,128)(2,1)} %param.16) | copy-start | bytes 49156
  192.9 112.4 %copy-start.6 = (bf16[128,64]{0,1:T(8,128)(2,1)S(1)}, bf16[128,64]{0,1:T(8,128)(2,1)}, u32[]{:S(2)}) copy-start(bf16[128,64]{0,1:T(8,128)(2,1)} %param.17) | copy-start | bytes 49156
  305.5 1.6 copy-start.2
  307.1 1.6 copy-start.3

commit v2 on v1

v2 whole, which is shorter than its diff:
```python
import functools

import jax
import jax.numpy as jnp
from jax import lax
from jax.experimental import pallas as pl
from jax.experimental.pallas import tpu as pltpu
from jax.sharding import PartitionSpec as P

MESH = pl.DeviceIdType.MESH
BF = jnp.bfloat16
F32 = jnp.float32
LOG2E = 1.4426950408889634
ORDERS = (("y", "z", "x"), ("z", "x", "y"), ("x", "y", "z"))
ROWS = ((0, 24), (24, 24), (48, 16))


def layer_norm(values):
    widened = values.astype(F32)
    average = jnp.mean(widened, axis=-1, keepdims=True)
    centred = widened - average
    variance = jnp.mean(centred * centred, axis=-1, keepdims=True)
    return (centred * lax.rsqrt(variance + 1e-05)).astype(BF)


def remote(src, dst, send, recv, device):
    return pltpu.make_async_remote_copy(
        src_ref=src, dst_ref=dst, send_sem=send, recv_sem=recv, device_id=device, device_id_type=MESH
    )


def embed_kernel(z_ref, sub_ref, lane_ref, wd_ref, wb_ref, pair_ref, bias_ref,
                 rs, rl, flat, s_send, s_recv, l_send, l_recv):
    row = lax.axis_index("row")
    col = lax.axis_index("col")
    slot = lax.rem(row, 2) * 8 + col
    target = row // 2
    barrier = pltpu.get_barrier_semaphore()

    def greet_row(d, _):
        pl.semaphore_signal(barrier, inc=1, device_id=(row, lax.rem(col + d, 8)), device_id_type=MESH)
        return 0

    lax.fori_loop(1, 8, greet_row, 0)

    def greet_source(s, _):
        src_row = 2 * col + s // 8
        src_col = lax.rem(s, 8)

        @pl.when(jnp.logical_or(src_row != row, src_col != col))
        def _():
            pl.semaphore_signal(barrier, inc=1, device_id=(src_row, src_col), device_id_type=MESH)

        return 0

    lax.fori_loop(0, 16, greet_source, 0)

    @pl.when(target == col)
    def _():
        pl.semaphore_wait(barrier, 22)

    @pl.when(target != col)
    def _():
        pl.semaphore_wait(barrier, 23)

    def row_copy(d):
        to = lax.rem(col + d, 8)
        return remote(sub_ref, rs.at[col], s_send.at[d - 1], s_recv.at[d - 1], (row, to))

    def lane_copy(r):
        return remote(lane_ref, rl.at[slot], l_send.at[r], l_recv.at[slot], (r, target))

    def lane_arrival(s):
        return remote(lane_ref, rl.at[s], l_send.at[s], l_recv.at[s], (2 * col + s // 8, lax.rem(s, 8)))

    def start_row(d, _):
        row_copy(d).start()
        return 0

    lax.fori_loop(1, 8, start_row, 0)

    def start_lane(r, _):
        @pl.when(jnp.logical_or(r != row, target != col))
        def _():
            lane_copy(r).start()

        return 0

    lax.fori_loop(0, 16, start_lane, 0)
    rs[col] = sub_ref[...]

    @pl.when(target == col)
    def _():
        rl[slot] = lane_ref[...]

    def wait_row(d, _):
        row_copy(d).wait()
        return 0

    lax.fori_loop(1, 8, wait_row, 0)

    def wait_lane(r, _):
        @pl.when(jnp.logical_or(r != row, target != col))
        def _():
            lane_copy(r).wait_send()

        @pl.when(jnp.logical_or(2 * col + r // 8 != row, lax.rem(r, 8) != col))
        def _():
            lane_arrival(r).wait_recv()

        return 0

    lax.fori_loop(0, 16, wait_lane, 0)

    lanes = jnp.sum(rl[...], axis=0)
    cx, cy, cz = lanes[0:1], lanes[1:2], lanes[2:3]
    edge = lax.broadcasted_iota(jnp.int32, (40, 128), 0)
    upper_edge = 27 + 4 * edge
    lower_edge = 23 + 4 * edge
    big = jnp.int32(1 << 20)
    lower = jnp.where(edge == 0, -1, jnp.where(edge == 39, big, lower_edge * lower_edge)).astype(F32)
    upper = jnp.where(edge >= 38, big, upper_edge * upper_edge).astype(F32)
    wd = wd_ref[...]
    wb = wb_ref[...]

    head = lax.broadcasted_iota(jnp.int32, (8, 128), 1) // 32

    def eight(t, _):
        own = rs[t]
        dx = own[:, 0:1] - cx
        dy = own[:, 1:2] - cy
        dz = own[:, 2:3] - cz
        squared = dx * dx + dy * dy + dz * dz
        key_bias = (own[:, 3:4] - 1.0) * 30000.0
        rows = []
        for a in range(8):
            i = t * 8 + a
            here = jnp.broadcast_to(squared[a : a + 1], (40, 128))
            hot = jnp.where(jnp.logical_and(here > lower, here <= upper), 1.0, 0.0).astype(BF)
            added = lax.dot_general(hot, wd, (((0,), (0,)), ((), ())), preferred_element_type=F32)
            pair = (z_ref[i].astype(F32) + added).astype(BF)
            flat[pl.ds(i, 128, stride=64), :] = pair.astype(F32)
            normed = layer_norm(pair)
            b = lax.dot_general(wb, normed, (((1,), (1,)), ((), ())), preferred_element_type=F32)
            rows.append(b + key_bias[a : a + 1])
        start = pl.multiple_of(t * 8, 8)
        by_head = [jnp.concatenate([r[h : h + 1] for r in rows], axis=0) for h in range(4)]
        for c in range(4):
            moved = [pltpu.roll(by_head[h], (32 * h - 32 * c) % 128, 1) for h in range(4)]
            block = moved[3]
            for h in (2, 1, 0):
                block = jnp.where(head == h, moved[h], block)
            bias_ref[c, pl.ds(start, 8), :] = block
        return 0

    lax.fori_loop(0, 8, eight, 0)

    def out(g, _):
        for j in range(8):
            at = pl.multiple_of((g * 8 + j) * 64, 64)
            pair_ref[g, j] = flat[pl.ds(at, 64), :].astype(BF)
        return 0

    lax.fori_loop(0, 16, out, 0)


def embed(z, sub, lane, wd, wb):
    return pl.pallas_call(
        embed_kernel,
        out_shape=(
            jax.ShapeDtypeStruct((16, 8, 64, 128), BF),
            jax.ShapeDtypeStruct((4, 64, 128), F32),
        ),
        in_specs=[pl.BlockSpec(memory_space=pltpu.VMEM)] * 5,
        out_specs=(pl.BlockSpec(memory_space=pltpu.VMEM),) * 2,
        scratch_shapes=[
            pltpu.VMEM((8, 8, 128), F32),
            pltpu.VMEM((16, 8, 128), F32),
            pltpu.VMEM((8192, 128), F32),
            pltpu.SemaphoreType.DMA((7,)),
            pltpu.SemaphoreType.DMA((7,)),
            pltpu.SemaphoreType.DMA((16,)),
            pltpu.SemaphoreType.DMA((16,)),
        ],
        compiler_params=pltpu.CompilerParams(collective_id=0, has_side_effects=True, vmem_limit_bytes=40 << 20),
        name="embed",
    )(z, sub, lane, wd, wb)


def place():
    row = lax.axis_index("row")
    col = lax.axis_index("col")
    core = lax.rem(row, 2)
    at = {"x": lax.rem(col, 4), "y": row // 4, "z": (col // 4) * 2 + lax.rem(row // 2, 2)}
    return row, col, core, at


def device_of(at, core):
    return (at["y"] * 4 + lax.rem(at["z"], 2) * 2 + core, (at["z"] // 2) * 4 + at["x"])


def beside(at, dim, delta):
    moved = dict(at)
    moved[dim] = lax.rem(at[dim] + delta + 4, 4)
    return moved


def of32(n):
    return pl.multiple_of(n, 32)


def main_kernel(pair_ref, bias_ref, wa_ref, wo_ref, d_ref, m_ref,
                xs, g0, g1, g2, q_s, k_s, v_s, g_s, s_s, u_s, relay,
                asend, arecv, osem, send, recv, lsem, psend, precv,
                dsend, drecv, rsend, rrecv, msend, mrecv, hsem):
    row, col, core, at = place()
    gs = (g0, g1, g2)
    zh = col // 4
    yh = row // 8
    partner = device_of(at, 1 - core)
    opposite = device_of(beside(at, "x", 2), core)
    looped = jnp.logical_and(yh == zh, core == yh)
    src_row0 = core * 8
    src_zh = yh
    slot = lax.rem(row, 8)
    barrier = pltpu.get_barrier_semaphore()

    def signal(device):
        pl.semaphore_signal(barrier, inc=1, device_id=device, device_id_type=MESH)

    def greet(d, _):
        signal((lax.rem(row + d, 16), col))
        return 0

    lax.fori_loop(1, 16, greet, 0)
    for dim in ("x", "y", "z"):
        for delta in (1, -1):
            signal(device_of(beside(at, dim, delta), core))
    signal(opposite)

    def greet_relay(s, _):
        @pl.when(jnp.logical_or(src_row0 + s != row, src_zh != zh))
        def _():
            signal((src_row0 + s, src_zh * 4 + at["x"]))

        return 0

    lax.fori_loop(0, 8, greet_relay, 0)

    @pl.when(looped)
    def _():
        pl.semaphore_wait(barrier, 29)

    @pl.when(jnp.logical_not(looped))
    def _():
        pl.semaphore_wait(barrier, 30)

    def a2a(d):
        to = lax.rem(row + d, 16)
        return remote(pair_ref.at[to], xs.at[row], asend.at[d - 1], arecv.at[d - 1], (to, col))

    def start_a2a(first, last):
        def go(d, _):
            a2a(d).start()
            return 0

        lax.fori_loop(first, last, go, 0)

    def gather_copy(stage, p, k, t):
        dims = ORDERS[p]
        first, count = ROWS[p]
        g = gs[p]
        delta = (1, -1)[k % 2]
        a = [at[d] for d in dims]
        if k >= 2:
            a[stage] = lax.rem(a[stage] - delta + 4, 4)
        a1, a2, a3 = a
        half = pl.ds(2 * (k % 2), 2)
        if stage == 0:
            dst = g.at[t, core, a3, a2, a1]
            src = bias_ref.at[t, pl.ds(first, count), :] if k < 2 else dst
            if k >= 2:
                part = pl.ds(0, 8) if k == 2 else pl.ds(8, count - 8)
                src = dst = dst.at[part]
        else:
            src = g.at[t, core, a3, a2] if stage == 1 else g.at[t, core, a3]
            if k >= 2:
                src = src.at[half]
            dst = src
        n = p * 12 + stage * 4 + k
        return remote(src, dst, send.at[t, n], recv.at[t, n], device_of(beside(at, dims[stage], delta), core))

    def keep(p, t):
        a1, a2, a3 = (at[d] for d in ORDERS[p])
        first, count = ROWS[p]
        return pltpu.make_async_copy(
            bias_ref.at[t, pl.ds(first, count), :], gs[p].at[t, core, a3, a2, a1], lsem.at[t, p]
        )

    def share(p, t):
        half = gs[p].at[t, core]
        return remote(half, half, psend.at[t, p], precv.at[t, p], partner)

    def gather_step(n, t):
        parts = range(3)
        if n == 0:
            for p in parts:
                keep(p, t).start()
                for k in (0, 1):
                    gather_copy(0, p, k, t).start()
        elif n in (1, 3, 5):
            stage = n // 2
            for p in parts:
                for k in (0, 1):
                    gather_copy(stage, p, k, t).wait_recv()
                    gather_copy(stage, p, k + 2, t).start()
        elif n in (2, 4):
            stage = n // 2
            for p in parts:
                if n == 2:
                    keep(p, t).wait()
                for k in (2, 3):
                    gather_copy(stage - 1, p, k, t).wait_recv()
                for k in (0, 1):
                    gather_copy(stage, p, k, t).start()
        elif n == 6:
            for p in parts:
                for k in (2, 3):
                    gather_copy(2, p, k, t).wait_recv()
                share(p, t).start()
        else:
            for p in parts:
                share(p, t).wait()
                for stage in range(3):
                    for k in range(4):
                        gather_copy(stage, p, k, t).wait_send()

    def direct(c, t):
        to = 2 * c + t // 2
        return (
            to,
            u_s.at[:, pl.ds(of32(c * 128 + t * 32), 32), :],
            d_ref.at[row, :, pl.ds(of32(lax.rem(t, 2) * 32), 32), :],
            dsend.at[t, c],
            drecv.at[lax.rem(t, 2), row],
        )

    def direct_remote(c, t):
        to, src, dst, s1, s2 = direct(c, t)
        return remote(src, dst, s1, s2, (to, col))

    def direct_local(c, t):
        to, src, dst, s1, s2 = direct(c, t)
        return pltpu.make_async_copy(src, dst, hsem.at[0, lax.rem(t, 2)])

    def direct_arrival(s, tt):
        return remote(
            u_s.at[:, pl.ds(0, 32), :], d_ref.at[s, :, pl.ds(of32(tt * 32), 32), :],
            dsend.at[0, 0], drecv.at[tt, s], (s, col),
        )

    def hop(delta, zz, t):
        x2 = lax.rem(at["x"] + delta, 4)
        c = zz * 4 + x2
        return remote(
            u_s.at[:, pl.ds(of32(c * 128 + t * 32), 32), :], relay.at[t, 3 - delta, zz],
            rsend.at[t, delta - 1, zz], rrecv.at[t, 3 - delta, zz], device_of(beside(at, "x", delta), core),
        )

    def hop_arrival(n, zz, t):
        return remote(
            u_s.at[:, pl.ds(0, 32), :], relay.at[t, n, zz],
            rsend.at[t, 2 - n, zz], rrecv.at[t, n, zz], device_of(beside(at, "x", n + 1), core),
        )

    def mirror(n, zz, t):
        sx = lax.rem(at["x"] + n, 4)
        to_row = 2 * (4 * zh + sx) + yh
        c = zz * 4 + at["x"]
        if n == 0:
            src = u_s.at[:, pl.ds(of32(c * 128 + t * 32), 32), :]
        else:
            src = relay.at[t, n - 1, zz]
        dst = m_ref.at[slot, :, pl.ds(of32(t * 32), 32), :]
        here = jnp.logical_and(to_row == row, zz == zh)
        rem = remote(src, dst, msend.at[t, n, zz], mrecv.at[t, slot], (to_row, c))
        loc = pltpu.make_async_copy(src, dst, hsem.at[1, t])
        return here, rem, loc

    def mirror_arrival(s, t):
        return remote(
            u_s.at[:, pl.ds(0, 32), :], m_ref.at[s, :, pl.ds(of32(t * 32), 32), :],
            msend.at[t, 0, 0], mrecv.at[t, s], (src_row0 + s, src_zh * 4 + at["x"]),
        )

    def either(here, if_here, otherwise):
        @pl.when(here)
        def _():
            if_here()

        @pl.when(jnp.logical_not(here))
        def _():
            otherwise()

    def exit_first(t):
        for zz in range(2):
            for delta in (1, 2, 3):
                hop(delta, zz, t).start()
        for zz in range(2):
            here, rem, loc = mirror(0, zz, t)
            either(here, loc.start, rem.start)

        def go(n, _):
            c = lax.rem(col + n, 8)
            either(
                2 * c + t // 2 == row, lambda: direct_local(c, t).start(), lambda: direct_remote(c, t).start()
            )
            return 0

        lax.fori_loop(0, 8, go, 0)

    def exit_second(t):
        for n in (1, 2, 3):
            for zz in range(2):
                hop_arrival(n - 1, zz, t).wait_recv()
                here, rem, loc = mirror(n, zz, t)
                either(here, loc.start, rem.start)

    def project(j):
        p = jnp.dot(layer_norm(xs[:, j].reshape(1024, 128)), wa_ref[...], preferred_element_type=F32)
        q_s[j] = (p[:, :128] * (32**-0.5)).astype(BF)
        k_s[j] = p[:, 128:256].astype(BF)
        v_s[j] = p[:, 256:384].astype(BF).T
        g_s[j] = p[:, 384:].astype(BF)

    head_of_lane = lax.broadcasted_iota(jnp.int32, (32, 128), 1) // 32
    ones = jnp.ones((16, 256), BF)

    def bias_block(t, cp, kb, n):
        parts = []
        for zl in range(2):
            for cc in range(2):
                for p in range(3):
                    where = {"x": 2 * lax.rem(cp, 2) + n, "y": kb, "z": 2 * (cp // 2) + zl}
                    d1, d2, d3 = ORDERS[p]
                    parts.append(gs[p][t, cc, where[d3], where[d2], where[d1]])
        return jnp.concatenate(parts, axis=0)

    def task(t, cp, j):
        parts = []
        for n in range(2):
            q = q_s[j, pl.ds(of32((cp * 2 + n) * 128 + t * 32), 32), :]
            for h in range(4):
                parts.append(jnp.where(head_of_lane == h, q, jnp.zeros_like(q)))
        qm = jnp.concatenate(parts, axis=0)
        mx = None
        for kb in range(4):
            s = lax.dot_general(k_s[j, pl.ds(kb * 256, 256), :], qm, (((1,), (1,)), ((), ())),
                                preferred_element_type=F32)
            s = s + jnp.concatenate([bias_block(t, cp, kb, 0), bias_block(t, cp, kb, 1)], axis=1)
            s_s[kb] = s
            m = jnp.max(s.reshape(32, 8, 256), axis=0)
            mx = m if mx is None else jnp.maximum(mx, m)
        m = jnp.max(mx, axis=0, keepdims=True)
        acc = None
        for kb in range(4):
            e = jnp.exp2(((s_s[kb] - m) * LOG2E).astype(BF))
            lhs = jnp.concatenate([v_s[j, :, kb * 256 : kb * 256 + 256], ones], axis=0)
            r = jnp.dot(lhs, e, preferred_element_type=F32)
            acc = r if acc is None else acc + r
        att = acc[:128] * (1.0 / acc[128:129])
        for n in range(2):
            a = att[:, n * 128 : n * 128 + 128].T
            rows = a[96:128]
            for h in (2, 1, 0):
                rows = jnp.where(head_of_lane == h, a[h * 32 : h * 32 + 32], rows)
            first = of32((cp * 2 + n) * 128 + t * 32)
            gate = g_s[j, pl.ds(first, 32), :].astype(F32)
            gated = (rows / (1.0 + jnp.exp(-gate))).astype(BF)
            upd = jnp.dot(gated, wo_ref[...], preferred_element_type=F32)
            x = xs[(cp * 2 + n) * 2 + t // 2, j, pl.ds(of32(lax.rem(t, 2) * 32), 32), :]
            u_s[j, pl.ds(first, 32), :] = (x.astype(F32) + upd).astype(BF)

    own = pltpu.make_async_copy(pair_ref.at[row], xs.at[row], osem)
    own.start()
    gather_step(0, 0)
    for n in range(1, 6):
        start_a2a(3 * n - 2, 3 * n + 1)
        gather_step(n, 0)
    own.wait()

    def wait_a2a(d, _):
        a2a(d).wait()
        return 0

    lax.fori_loop(1, 16, wait_a2a, 0)
    gather_step(6, 0)

    def prepare(j, _):
        for n in range(8):
            @pl.when(j == n)
            def _():
                gather_step(n, 1)

        project(j)
        return 0

    lax.fori_loop(0, 8, prepare, 0)
    gather_step(7, 0)

    def chunk(t, _):
        def half(hh, _):
            for n in range(8):
                @pl.when(jnp.logical_and(hh == n, t < 2))
                def _():
                    gather_step(n, t + 2)

            @pl.when(jnp.logical_and(hh == 0, t > 0))
            def _():
                exit_first(t - 1)

            @pl.when(jnp.logical_and(hh == 3, t > 0))
            def _():
                exit_second(t - 1)

            def column(j, _):
                task(t, hh // 2, lax.rem(hh, 2) * 4 + j)
                return 0

            lax.fori_loop(0, 4, column, 0)
            return 0

        lax.fori_loop(0, 8, half, 0)
        return 0

    lax.fori_loop(0, 4, chunk, 0)
    exit_first(3)
    exit_second(3)

    def drain(t, _):
        def one(c, _):
            either(
                2 * c + t // 2 == row, lambda: direct_local(c, t).wait(), lambda: direct_remote(c, t).wait_send()
            )
            return 0

        lax.fori_loop(0, 8, one, 0)
        for zz in range(2):
            for delta in (1, 2, 3):
                hop(delta, zz, t).wait_send()
            for n in range(4):
                here, rem, loc = mirror(n, zz, t)
                either(here, loc.wait, rem.wait_send)

        def arrived(s, _):
            @pl.when(jnp.logical_or(src_row0 + s != row, src_zh != zh))
            def _():
                mirror_arrival(s, t).wait_recv()

            return 0

        lax.fori_loop(0, 8, arrived, 0)
        return 0

    lax.fori_loop(0, 4, drain, 0)

    def landed(s, _):
        @pl.when(s != row)
        def _():
            for tt in range(2):
                direct_arrival(s, tt).wait_recv()

        return 0

    lax.fori_loop(0, 16, landed, 0)


def main(pair, bias, wa, wo):
    any_spec = pl.BlockSpec(memory_space=pl.ANY)
    vmem = pl.BlockSpec(memory_space=pltpu.VMEM)
    dma = pltpu.SemaphoreType.DMA
    return pl.pallas_call(
        main_kernel,
        out_shape=(jax.ShapeDtypeStruct((16, 8, 64, 128), BF), jax.ShapeDtypeStruct((8, 8, 128, 128), BF)),
        in_specs=[any_spec, vmem, vmem, vmem],
        out_specs=(any_spec,) * 2,
        scratch_shapes=[pltpu.VMEM((16, 8, 64, 128), BF)]
        + [pltpu.VMEM((4, 2, 4, 4, 4, n, 128), F32) for _, n in ROWS]
        + [
            pltpu.VMEM((8, 1024, 128), BF),
            pltpu.VMEM((8, 1024, 128), BF),
            pltpu.VMEM((8, 128, 1024), BF),
            pltpu.VMEM((8, 1024, 128), BF),
            pltpu.VMEM((4, 256, 256), F32),
            pltpu.VMEM((8, 1024, 128), BF),
            pltpu.VMEM((4, 3, 2, 8, 32, 128), BF),
            dma((15,)), dma((15,)), dma,
            dma((4, 36)), dma((4, 36)), dma((4, 3)), dma((4, 3)), dma((4, 3)),
            dma((4, 8)), dma((2, 16)), dma((4, 3, 2)), dma((4, 3, 2)), dma((4, 4, 2)), dma((4, 8)), dma((2, 4)),
        ],
        compiler_params=pltpu.CompilerParams(collective_id=1, has_side_effects=True, vmem_limit_bytes=60 << 20),
        name="main",
    )(pair, bias, wa, wo)


def logits_kernel(d_ref, m_ref, wp_ref, we_ref, o_ref, flat):
    step = pl.program_id(0)

    @pl.when(step == 0)
    def _():
        def widen(g, _):
            for j in range(8):
                at = pl.multiple_of((g * 8 + j) * 64, 64)
                flat[pl.ds(at, 64), :] = d_ref[g, j].astype(F32)
            return 0

        lax.fori_loop(0, 16, widen, 0)

    for a in range(8):
        u = flat[pl.ds(step * 8 + a, 128, stride=64), :]
        sym = u + m_ref[a].astype(F32)
        pae = jnp.dot(layer_norm(u), wp_ref[...], preferred_element_type=F32)
        pde = jnp.dot(layer_norm(sym), we_ref[...], preferred_element_type=F32)
        o_ref[a] = pae + pde


def logits(d, m, wp, we):
    return pl.pallas_call(
        logits_kernel,
        grid=(8,),
        out_shape=jax.ShapeDtypeStruct((64, 128, 128), F32),
        in_specs=[
            pl.BlockSpec((16, 8, 64, 128), lambda t: (0, 0, 0, 0)),
            pl.BlockSpec((8, 128, 128), lambda t: (t, 0, 0)),
            pl.BlockSpec((128, 128), lambda t: (0, 0)),
            pl.BlockSpec((128, 128), lambda t: (0, 0)),
        ],
        out_specs=pl.BlockSpec((8, 128, 128), lambda t: (t, 0, 0)),
        scratch_shapes=[pltpu.VMEM((8192, 128), F32)],
        compiler_params=pltpu.CompilerParams(vmem_limit_bytes=40 << 20),
        name="logits",
    )(d, m, wp, we)


def per_device(z_trunk, coords, token_mask, w_dist, w_attn, w_bias, w_out, w_pae, w_pde):
    device = lax.axis_index("row") * 8 + lax.axis_index("col")
    info = jnp.concatenate([coords, token_mask[None]], axis=0).astype(F32)
    sub = jnp.pad(info.T, ((0, 0), (0, 124)))
    lane = jnp.arange(128, dtype=jnp.int32)[None, :] // 8 == lax.rem(device, 16)
    lane = jnp.where(lane, jnp.tile(info, (2, 16)), 0.0)
    wd = jnp.pad(w_dist, ((0, 1), (0, 0)))
    wb = jnp.pad(w_bias.T, ((0, 4), (0, 0)))
    pair, bias = embed(z_trunk, sub, lane, wd, wb)
    direct, mirror = main(pair, bias, w_attn, w_out)
    wp = jnp.pad(w_pae, ((0, 0), (0, 64)))
    we = jnp.pad(w_pde, ((0, 0), (64, 0)))
    return logits(direct, mirror.reshape(64, 128, 128), wp, we)


def solution(mesh):
    in_specs = (P("row", "col", None), P(None, ("row", "col")), P(("row", "col")), P(), P(), P(), P(), P(), P())
    return jax.shard_map(
        per_device, mesh=mesh, in_specs=in_specs, out_specs=P("row", "col", None), check_vma=False
    )
```

time: 320 us -> 306 us (0.956)
  the two profiles are of different devices: /device:TPU:97 before, /device:TPU:31 now
where the time goes in v2:
time: 306 us; the launch traced here: 305 us
  Pallas kernels  293 us (96%)
  local copies, waits for them, and re-layouts  11.5 us (4%)
    pallas_call x1, Pallas kernels, main(): pl.pallas_call(main_kernel, out_shape=(jax.ShapeDtypeStruct((16, 8, 64, 1...  252 us
    pallas_call x1, Pallas kernels, embed(): pl.pallas_call(embed_kernel, out_shape=(jax.ShapeDtypeStruct((16, 8, 64,...  29.7 us
    pallas_call x1, Pallas kernels, logits(): pl.pallas_call(logits_kernel, grid=(8,), out_shape=jax.ShapeDtypeStruct((...  11.3 us
    unnamed x13, local copies, waits for them, and re-layouts  9.12 us

profile of v2, /device:TPU:31, one launch (start us, length us, event | category | flops | bytes accessed | tf_op | source)
XLA Modules:
  0.0 304.8 jit_solution(737138857927805544)
XLA Ops:
  0.0 0.7 pad.22.wb_ref
  0.7 0.8 copy.15
  1.4 0.7 copy.16
  2.2 0.1 fusion.1
  2.3 0.1 add_convert_fusion
  2.3 0.1 copy.17
  2.4 0.7 pad.21.wd_ref
  3.1 0.8 copy.18
  4.0 0.8 copy.19
  4.8 0.1 pad.24.we_ref
  4.9 0.1 tile.10
  5.0 0.0 copy-start.1
  5.0 1.6 copy-done.1
  6.6 29.7 %embed.1 = (bf16[16,8,64,128]{3,2,1,0:T(8,128)(2,1)S(1)}, f32[4,64,128]{2,1,0:T(8,128)S(1)}) custom-call(bf16[64,128,128]{2,1,0:T(8,128)(2,1)S(1)} %copy-done.1, f32[8,128]{1,0:T(8,128)S(1)} %pad.20.sub_ref, f32[8,128]{1,0:T(8,128)S(1)} %broadcast_select_fusion.lane_ref, bf16[40,128]{1,0:T(8,128)(2,1)S(1)} %pad.21.wd_ref, bf16[8,128]{1,0:T(8,128)(2,1)S(1)} %pad.22.wb_ref), custom_call_target="tpu_custom_call" | custom-call | tf_op jit(solution)/shard_map/embed/pallas_call | solution.py:168
  36.3 0.0 copy-start
  36.3 1.3 copy-done
  37.7 0.0 copy-start.4
  37.7 0.6 copy-done.4
  38.3 252.0 %main.1 = (bf16[16,8,64,128]{3,2,1,0:T(8,128)(2,1)}, bf16[8,8,128,128]{3,2,1,0:T(8,128)(2,1)}) custom-call(bf16[16,8,64,128]{3,2,1,0:T(8,128)(2,1)} %copy-done, f32[4,64,128]{2,1,0:T(8,128)} %copy-done.4, bf16[128,512]{1,0:T(8,128)(2,1)} %wa_ref.1, bf16[128,128]{1,0:T(8,128)(2,1)} %wo_ref.1), custom_call_target="tpu_custom_call" | custom-call | tf_op jit(solution)/shard_map/main/pallas_call | solution.py:582
  290.3 0.0 copy-start.2
  290.3 1.6 copy-done.2
  291.9 0.0 copy-start.3
  291.9 1.6 copy-done.3
  293.5 11.3 %logits.1 = f32[64,128,128]{2,1,0:T(8,128)} custom-call(bf16[16,8,64,128]{3,2,1,0:T(8,128)(2,1)S(1)} %copy-done.2, bf16[64,128,128]{2,1,0:T(8,128)(2,1)S(1)} %bitcast.7, bf16[128,128]{1,0:T(8,128)(2,1)S(1)} %pad.23.wp_ref, bf16[128,128]{1,0:T(8,128)(2,1)S(1)} %pad.24.we_ref), custom_call_target="tpu_custom_call" | custom-call | tf_op jit(solution)/shard_map/logits/pallas_call | solution.py:628
  (5 shorter events, 0.0 us)
Async XLA Ops:
  5.0 1.6 copy-start.1
  36.3 1.3 copy-start
  37.7 0.6 copy-start.4
  290.3 1.6 copy-start.2
  291.9 1.6 copy-start.3

commit v3 on v2

--- a/solution.py
+++ b/solution.py
@@ -13,6 +13,16 @@
 LOG2E = 1.4426950408889634
 ORDERS = (("y", "z", "x"), ("z", "x", "y"), ("x", "y", "z"))
 ROWS = ((0, 24), (24, 24), (48, 16))
+SPREAD = (
+    (1, 0, 0), (3, 0, 0), (0, 1, 0), (2, 0, 0), (1, 1, 0), (3, 1, 0), (0, 0, 1), (2, 1, 0),
+    (1, 0, 1), (3, 0, 1), (0, 1, 1), (2, 0, 1), (1, 1, 1), (3, 1, 1), (2, 1, 1),
+)
+PREPARE = {0: (1, 3), 2: (2, 0), 4: (1, 4), 6: (2, 1)}
+ATTEND = {
+    (0, 0): (1, 5), (0, 1): (2, 2), (0, 2): (1, 6), (0, 3): (2, 3), (0, 4): (1, 7), (0, 5): (2, 4), (0, 6): (3, 0),
+    (0, 7): (2, 5), (1, 0): (3, 1), (1, 1): (2, 6), (1, 2): (3, 2), (1, 3): (2, 7), (1, 4): (3, 3), (1, 6): (3, 4),
+    (2, 0): (3, 5), (2, 2): (3, 6), (2, 4): (3, 7),
+}
 
 
 def layer_norm(values):
@@ -210,7 +220,7 @@
 
 
 def main_kernel(pair_ref, bias_ref, wa_ref, wo_ref, d_ref, m_ref,
-                xs, g0, g1, g2, q_s, k_s, v_s, g_s, s_s, u_s, relay,
+                xs, g0, g1, g2, q_s, k_s, v_s, g_s, s_s, m_s, acc_s, u_s, relay,
                 asend, arecv, osem, send, recv, lsem, psend, precv,
                 dsend, drecv, rsend, rrecv, msend, mrecv, hsem):
     row, col, core, at = place()
@@ -255,16 +265,10 @@
     def _():
         pl.semaphore_wait(barrier, 30)
 
-    def a2a(d):
-        to = lax.rem(row + d, 16)
-        return remote(pair_ref.at[to], xs.at[row], asend.at[d - 1], arecv.at[d - 1], (to, col))
-
-    def start_a2a(first, last):
-        def go(d, _):
-            a2a(d).start()
-            return 0
-
-        lax.fori_loop(first, last, go, 0)
+    def a2a(n):
+        dy, dz, dc = SPREAD[n]
+        to = lax.rem(at["y"] + dy, 4) * 4 + lax.rem(lax.rem(row // 2, 2) + dz, 2) * 2 + lax.rem(core + dc, 2)
+        return remote(pair_ref.at[to], xs.at[row], asend.at[n], arecv.at[n], (to, col))
 
     def gather_copy(stage, p, k, t):
         dims = ORDERS[p]
@@ -446,94 +450,131 @@
                     parts.append(gs[p][t, cc, where[d3], where[d2], where[d1]])
         return jnp.concatenate(parts, axis=0)
 
-    def task(t, cp, j):
+    diagonal = lax.broadcasted_iota(jnp.int32, (128, 256), 0) // 32 == lax.rem(
+        lax.broadcasted_iota(jnp.int32, (128, 256), 1) // 32, 4
+    )
+    fold_row = lax.broadcasted_iota(jnp.int32, (64, 256), 0)
+    fold_lane = lax.broadcasted_iota(jnp.int32, (64, 256), 1)
+    fold = jnp.where(
+        jnp.logical_and(fold_row // 32 == fold_lane // 128, lax.rem(fold_row, 32) == lax.rem(fold_lane, 32)), 1.0, 0.0
+    ).astype(BF)
+    minor = (((1,), (1,)), ((), ()))
+
+    def split(f):
+        return f // 32, lax.rem(f, 32) // 8, lax.rem(f, 8)
+
+    def queries(t, cp, j):
         parts = []
         for n in range(2):
             q = q_s[j, pl.ds(of32((cp * 2 + n) * 128 + t * 32), 32), :]
             for h in range(4):
                 parts.append(jnp.where(head_of_lane == h, q, jnp.zeros_like(q)))
-        qm = jnp.concatenate(parts, axis=0)
-        mx = None
+        return jnp.concatenate(parts, axis=0)
+
+    def score(t, cp, j, qm, kb):
+        s = lax.dot_general(k_s[j, pl.ds(kb * 256, 256), :], qm, minor, preferred_element_type=F32)
+        return s + jnp.concatenate([bias_block(t, cp, kb, 0), bias_block(t, cp, kb, 1)], axis=1)
+
+    def score_block(b, t, cp, j, qm, kb, highest):
+        s = score(t, cp, j, qm, kb)
+        s_s[b, kb] = s
+        here = jnp.max(s.reshape(32, 8, 256), axis=0)
+        return here if highest is None else jnp.maximum(highest, here)
+
+    def finish(t, cp, j, acc):
+        att = jnp.where(diagonal, acc[:128] * (1.0 / acc[128:129]), 0.0)
+        high = att.astype(BF)
+        low = (att - high.astype(F32)).astype(BF)
+        rows = lax.dot_general(fold, high, minor, preferred_element_type=F32)
+        rows = rows + lax.dot_general(fold, low, minor, preferred_element_type=F32)
+        firsts = [of32((cp * 2 + n) * 128 + t * 32) for n in range(2)]
+        gate = jnp.concatenate([g_s[j, pl.ds(first, 32), :] for first in firsts], axis=0).astype(F32)
+        gated = (rows / (1.0 + jnp.exp(-gate))).astype(BF)
+        upd = jnp.dot(gated, wo_ref[...], preferred_element_type=F32)
+        for n, first in enumerate(firsts):
+            x = xs[(cp * 2 + n) * 2 + t // 2, j, pl.ds(of32(lax.rem(t, 2) * 32), 32), :]
+            u_s[j, pl.ds(first, 32), :] = (x.astype(F32) + upd[n * 32 : n * 32 + 32]).astype(BF)
+
+    def prologue():
+        highest = None
+        qm = queries(0, 0, 0)
         for kb in range(4):
-            s = lax.dot_general(k_s[j, pl.ds(kb * 256, 256), :], qm, (((1,), (1,)), ((), ())),
-                                preferred_element_type=F32)
-            s = s + jnp.concatenate([bias_block(t, cp, kb, 0), bias_block(t, cp, kb, 1)], axis=1)
-            s_s[kb] = s
-            m = jnp.max(s.reshape(32, 8, 256), axis=0)
-            mx = m if mx is None else jnp.maximum(mx, m)
-        m = jnp.max(mx, axis=0, keepdims=True)
+            highest = score_block(0, 0, 0, 0, qm, kb, highest)
+        m_s[0] = highest
+
+    def task(f, b):
+        t, cp, j = split(f)
+        t2, cp2, j2 = split(jnp.minimum(f + 1, 127))
+        t0, cp0, j0 = split(jnp.maximum(f - 1, 0))
+        qm = queries(t2, cp2, j2)
+        m = jnp.max(m_s[b], axis=0, keepdims=True)
         acc = None
+        highest = None
         for kb in range(4):
-            e = jnp.exp2(((s_s[kb] - m) * LOG2E).astype(BF))
+            e = jnp.exp2((s_s[b, kb] - m) * LOG2E).astype(BF)
+            highest = score_block(1 - b, t2, cp2, j2, qm, kb, highest)
             lhs = jnp.concatenate([v_s[j, :, kb * 256 : kb * 256 + 256], ones], axis=0)
             r = jnp.dot(lhs, e, preferred_element_type=F32)
             acc = r if acc is None else acc + r
-        att = acc[:128] * (1.0 / acc[128:129])
-        for n in range(2):
-            a = att[:, n * 128 : n * 128 + 128].T
-            rows = a[96:128]
-            for h in (2, 1, 0):
-                rows = jnp.where(head_of_lane == h, a[h * 32 : h * 32 + 32], rows)
-            first = of32((cp * 2 + n) * 128 + t * 32)
-            gate = g_s[j, pl.ds(first, 32), :].astype(F32)
-            gated = (rows / (1.0 + jnp.exp(-gate))).astype(BF)
-            upd = jnp.dot(gated, wo_ref[...], preferred_element_type=F32)
-            x = xs[(cp * 2 + n) * 2 + t // 2, j, pl.ds(of32(lax.rem(t, 2) * 32), 32), :]
-            u_s[j, pl.ds(first, 32), :] = (x.astype(F32) + upd).astype(BF)
+            if kb == 1:
+                finish(t0, cp0, j0, acc_s[1 - b])
+        m_s[1 - b] = highest
+        acc_s[b] = acc
 
     own = pltpu.make_async_copy(pair_ref.at[row], xs.at[row], osem)
     own.start()
     gather_step(0, 0)
-    for n in range(1, 6):
-        start_a2a(3 * n - 2, 3 * n + 1)
+    for n in range(1, 8):
+        for d in range(3 * n - 3, min(3 * n, 15)):
+            a2a(d).start()
         gather_step(n, 0)
+        if n in (2, 4, 6):
+            gather_step(n // 2 - 1, 1)
     own.wait()
-
-    def wait_a2a(d, _):
-        a2a(d).wait()
-        return 0
-
-    lax.fori_loop(1, 16, wait_a2a, 0)
-    gather_step(6, 0)
+    for n in range(15):
+        a2a(n).wait()
 
     def prepare(j, _):
-        for n in range(8):
+        for n, (chunk, step) in PREPARE.items():
             @pl.when(j == n)
             def _():
-                gather_step(n, 1)
+                gather_step(step, chunk)
 
         project(j)
         return 0
 
     lax.fori_loop(0, 8, prepare, 0)
-    gather_step(7, 0)
 
     def chunk(t, _):
         def half(hh, _):
-            for n in range(8):
-                @pl.when(jnp.logical_and(hh == n, t < 2))
+            for (tt, n), (later, step) in ATTEND.items():
+                @pl.when(jnp.logical_and(hh == n, t == tt))
                 def _():
-                    gather_step(n, t + 2)
-
-            @pl.when(jnp.logical_and(hh == 0, t > 0))
+                    gather_step(step, later)
+
+            @pl.when(jnp.logical_and(hh == 1, t > 0))
             def _():
                 exit_first(t - 1)
 
-            @pl.when(jnp.logical_and(hh == 3, t > 0))
+            @pl.when(jnp.logical_and(hh == 4, t > 0))
             def _():
                 exit_second(t - 1)
 
-            def column(j, _):
-                task(t, hh // 2, lax.rem(hh, 2) * 4 + j)
+            def two(i, _):
+                task(t * 32 + hh * 4 + i * 2, 0)
+                task(t * 32 + hh * 4 + i * 2 + 1, 1)
                 return 0
 
-            lax.fori_loop(0, 4, column, 0)
+            lax.fori_loop(0, 2, two, 0)
             return 0
 
         lax.fori_loop(0, 8, half, 0)
         return 0
 
+    prologue()
+    acc_s[1] = jnp.ones((144, 256), F32)
     lax.fori_loop(0, 4, chunk, 0)
+    finish(3, 3, 7, acc_s[1])
     exit_first(3)
     exit_second(3)
 
@@ -591,7 +632,9 @@
             pltpu.VMEM((8, 1024, 128), BF),
             pltpu.VMEM((8, 128, 1024), BF),
             pltpu.VMEM((8, 1024, 128), BF),
-            pltpu.VMEM((4, 256, 256), F32),
+            pltpu.VMEM((2, 4, 256, 256), F32),
+            pltpu.VMEM((2, 8, 256), F32),
+            pltpu.VMEM((2, 144, 256), F32),
             pltpu.VMEM((8, 1024, 128), BF),
             pltpu.VMEM((4, 3, 2, 8, 32, 128), BF),
             dma((15,)), dma((15,)), dma,

time: 306 us -> 234 us (0.76)
  Pallas kernels: 293 us -> 221 us
    pallas_call x1, Pallas kernels: 252 us -> 180 us  [main(): pl.pallas_call(main_kernel, out_shape=(jax.ShapeDtypeStruct((16, 8, 64, 1...]
where the time goes in v3:
time: 234 us; the launch traced here: 232 us
  Pallas kernels  221 us (94%)
  local copies, waits for them, and re-layouts  11.5 us (5%)
    pallas_call x1, Pallas kernels, main(): pl.pallas_call(main_kernel, out_shape=(jax.ShapeDtypeStruct((16, 8, 64, 1...  180 us
    pallas_call x1, Pallas kernels, embed(): pl.pallas_call(embed_kernel, out_shape=(jax.ShapeDtypeStruct((16, 8, 64,...  29.7 us
    pallas_call x1, Pallas kernels, logits(): pl.pallas_call(logits_kernel, grid=(8,), out_shape=jax.ShapeDtypeStruct((...  11.3 us
    unnamed x13, local copies, waits for them, and re-layouts  9.12 us

profile of v3, /device:TPU:31, one launch (start us, length us, event | category | flops | bytes accessed | tf_op | source)
XLA Modules:
  0.0 232.4 jit_solution(17058976472291022631)
XLA Ops:
  0.0 0.7 pad.22.wb_ref
  0.7 0.8 copy.15
  1.4 0.7 copy.16
  2.2 0.1 fusion.1
  2.3 0.1 add_convert_fusion
  2.3 0.1 copy.17
  2.4 0.7 pad.21.wd_ref
  3.1 0.8 copy.18
  4.0 0.8 copy.19
  4.8 0.1 pad.24.we_ref
  4.9 0.1 tile.10
  5.0 0.0 copy-start.1
  5.0 1.6 copy-done.1
  6.6 29.7 %embed.1 = (bf16[16,8,64,128]{3,2,1,0:T(8,128)(2,1)S(1)}, f32[4,64,128]{2,1,0:T(8,128)S(1)}) custom-call(bf16[64,128,128]{2,1,0:T(8,128)(2,1)S(1)} %copy-done.1, f32[8,128]{1,0:T(8,128)S(1)} %pad.20.sub_ref, f32[8,128]{1,0:T(8,128)S(1)} %broadcast_select_fusion.lane_ref, bf16[40,128]{1,0:T(8,128)(2,1)S(1)} %pad.21.wd_ref, bf16[8,128]{1,0:T(8,128)(2,1)S(1)} %pad.22.wb_ref), custom_call_target="tpu_custom_call" | custom-call | tf_op jit(solution)/shard_map/embed/pallas_call | solution.py:178
  36.3 0.0 copy-start
  36.3 1.3 copy-done
  37.7 0.0 copy-start.4
  37.7 0.6 copy-done.4
  38.3 179.6 %main.1 = (bf16[16,8,64,128]{3,2,1,0:T(8,128)(2,1)}, bf16[8,8,128,128]{3,2,1,0:T(8,128)(2,1)}) custom-call(bf16[16,8,64,128]{3,2,1,0:T(8,128)(2,1)} %copy-done, f32[4,64,128]{2,1,0:T(8,128)} %copy-done.4, bf16[128,512]{1,0:T(8,128)(2,1)} %wa_ref.1, bf16[128,128]{1,0:T(8,128)(2,1)} %wo_ref.1), custom_call_target="tpu_custom_call" | custom-call | tf_op jit(solution)/shard_map/main/pallas_call | solution.py:623
  217.9 0.0 copy-start.2
  217.9 1.6 copy-done.2
  219.5 0.0 copy-start.3
  219.5 1.6 copy-done.3
  221.1 11.3 %logits.1 = f32[64,128,128]{2,1,0:T(8,128)} custom-call(bf16[16,8,64,128]{3,2,1,0:T(8,128)(2,1)S(1)} %copy-done.2, bf16[64,128,128]{2,1,0:T(8,128)(2,1)S(1)} %bitcast.7, bf16[128,128]{1,0:T(8,128)(2,1)S(1)} %pad.23.wp_ref, bf16[128,128]{1,0:T(8,128)(2,1)S(1)} %pad.24.we_ref), custom_call_target="tpu_custom_call" | custom-call | tf_op jit(solution)/shard_map/logits/pallas_call | solution.py:671
  (5 shorter events, 0.0 us)
Async XLA Ops:
  5.0 1.6 copy-start.1
  36.3 1.3 copy-start
  37.7 0.6 copy-start.4
  217.9 1.6 copy-start.2
  219.5 1.6 copy-start.3

commit v4 on v3

--- a/solution.py
+++ b/solution.py
@@ -17,11 +17,10 @@
     (1, 0, 0), (3, 0, 0), (0, 1, 0), (2, 0, 0), (1, 1, 0), (3, 1, 0), (0, 0, 1), (2, 1, 0),
     (1, 0, 1), (3, 0, 1), (0, 1, 1), (2, 0, 1), (1, 1, 1), (3, 1, 1), (2, 1, 1),
 )
-PREPARE = {0: (1, 3), 2: (2, 0), 4: (1, 4), 6: (2, 1)}
+PREPARE = {0: (1, 3), 1: (2, 0), 5: (0, 5), 7: (2, 1)}
 ATTEND = {
-    (0, 0): (1, 5), (0, 1): (2, 2), (0, 2): (1, 6), (0, 3): (2, 3), (0, 4): (1, 7), (0, 5): (2, 4), (0, 6): (3, 0),
-    (0, 7): (2, 5), (1, 0): (3, 1), (1, 1): (2, 6), (1, 2): (3, 2), (1, 3): (2, 7), (1, 4): (3, 3), (1, 6): (3, 4),
-    (2, 0): (3, 5), (2, 2): (3, 6), (2, 4): (3, 7),
+    (0, 0): (1, 4), (0, 2): (2, 2), (0, 3): (3, 0), (0, 4): (1, 5), (0, 5): (2, 3), (0, 6): (3, 1),
+    (1, 0): (2, 4), (1, 1): (3, 2), (1, 3): (2, 5), (1, 4): (3, 3), (1, 7): (3, 4), (2, 2): (3, 5),
 }
 
 
@@ -123,38 +122,39 @@
     lax.fori_loop(0, 16, wait_lane, 0)
 
     lanes = jnp.sum(rl[...], axis=0)
-    cx, cy, cz = lanes[0:1], lanes[1:2], lanes[2:3]
-    edge = lax.broadcasted_iota(jnp.int32, (40, 128), 0)
+    turned = jnp.concatenate([lanes] * 16, axis=0).T
+    cx, cy, cz = (jnp.broadcast_to(turned[:, n : n + 1], (128, 128)) for n in range(3))
+    edge = lax.broadcasted_iota(jnp.int32, (1, 128), 1)
     upper_edge = 27 + 4 * edge
     lower_edge = 23 + 4 * edge
     big = jnp.int32(1 << 20)
-    lower = jnp.where(edge == 0, -1, jnp.where(edge == 39, big, lower_edge * lower_edge)).astype(F32)
+    lower = jnp.where(edge == 0, -1, jnp.where(edge >= 39, big, lower_edge * lower_edge)).astype(F32)
     upper = jnp.where(edge >= 38, big, upper_edge * upper_edge).astype(F32)
-    wd = wd_ref[...]
-    wb = wb_ref[...]
-
     head = lax.broadcasted_iota(jnp.int32, (8, 128), 1) // 32
 
     def eight(t, _):
         own = rs[t]
-        dx = own[:, 0:1] - cx
-        dy = own[:, 1:2] - cy
-        dz = own[:, 2:3] - cz
-        squared = dx * dx + dy * dy + dz * dz
         key_bias = (own[:, 3:4] - 1.0) * 30000.0
-        rows = []
+        hots = []
         for a in range(8):
-            i = t * 8 + a
-            here = jnp.broadcast_to(squared[a : a + 1], (40, 128))
-            hot = jnp.where(jnp.logical_and(here > lower, here <= upper), 1.0, 0.0).astype(BF)
-            added = lax.dot_general(hot, wd, (((0,), (0,)), ((), ())), preferred_element_type=F32)
-            pair = (z_ref[i].astype(F32) + added).astype(BF)
-            flat[pl.ds(i, 128, stride=64), :] = pair.astype(F32)
-            normed = layer_norm(pair)
-            b = lax.dot_general(wb, normed, (((1,), (1,)), ((), ())), preferred_element_type=F32)
-            rows.append(b + key_bias[a : a + 1])
+            dx = cx - own[a : a + 1, 0:1]
+            dy = cy - own[a : a + 1, 1:2]
+            dz = cz - own[a : a + 1, 2:3]
+            squared = dx * dx + dy * dy + dz * dz
+            hots.append(jnp.where(jnp.logical_and(squared > lower, squared <= upper), 1.0, 0.0).astype(BF))
+        added = jnp.dot(jnp.concatenate(hots, axis=0), wd_ref[...], preferred_element_type=F32)
         start = pl.multiple_of(t * 8, 8)
-        by_head = [jnp.concatenate([r[h : h + 1] for r in rows], axis=0) for h in range(4)]
+        z = z_ref[pl.ds(start, 8)].reshape(1024, 128).astype(F32)
+        pair = (z + added).astype(BF)
+        wide = pair.astype(F32)
+        for a in range(8):
+            flat[pl.ds(start + a, 128, stride=64), :] = wide[a * 128 : a * 128 + 128]
+        normed = layer_norm(pair)
+        b = lax.dot_general(wb_ref[...], normed, (((1,), (1,)), ((), ())), preferred_element_type=F32)
+        by_head = [
+            jnp.concatenate([b[h : h + 1, a * 128 : a * 128 + 128] for a in range(8)], axis=0) + key_bias
+            for h in range(4)
+        ]
         for c in range(4):
             moved = [pltpu.roll(by_head[h], (32 * h - 32 * c) % 128, 1) for h in range(4)]
             block = moved[3]
@@ -163,7 +163,7 @@
             bias_ref[c, pl.ds(start, 8), :] = block
         return 0
 
-    lax.fori_loop(0, 8, eight, 0)
+    lax.fori_loop(0, 8, eight, 0, unroll=4)
 
     def out(g, _):
         for j in range(8):
@@ -228,7 +228,6 @@
     zh = col // 4
     yh = row // 8
     partner = device_of(at, 1 - core)
-    opposite = device_of(beside(at, "x", 2), core)
     looped = jnp.logical_and(yh == zh, core == yh)
     src_row0 = core * 8
     src_zh = yh
@@ -246,7 +245,8 @@
     for dim in ("x", "y", "z"):
         for delta in (1, -1):
             signal(device_of(beside(at, dim, delta), core))
-    signal(opposite)
+    signal(device_of(beside(at, "x", 2), core))
+    signal(device_of(beside(at, "z", 2), core))
 
     def greet_relay(s, _):
         @pl.when(jnp.logical_or(src_row0 + s != row, src_zh != zh))
@@ -259,11 +259,11 @@
 
     @pl.when(looped)
     def _():
-        pl.semaphore_wait(barrier, 29)
+        pl.semaphore_wait(barrier, 30)
 
     @pl.when(jnp.logical_not(looped))
     def _():
-        pl.semaphore_wait(barrier, 30)
+        pl.semaphore_wait(barrier, 31)
 
     def a2a(n):
         dy, dz, dc = SPREAD[n]
@@ -274,24 +274,20 @@
         dims = ORDERS[p]
         first, count = ROWS[p]
         g = gs[p]
-        delta = (1, -1)[k % 2]
+        delta = (1, -1, 2)[k] if stage < 2 else (1, -1)[k % 2]
         a = [at[d] for d in dims]
-        if k >= 2:
+        if stage == 2 and k >= 2:
             a[stage] = lax.rem(a[stage] - delta + 4, 4)
         a1, a2, a3 = a
-        half = pl.ds(2 * (k % 2), 2)
         if stage == 0:
+            src = bias_ref.at[t, pl.ds(first, count), :]
             dst = g.at[t, core, a3, a2, a1]
-            src = bias_ref.at[t, pl.ds(first, count), :] if k < 2 else dst
-            if k >= 2:
-                part = pl.ds(0, 8) if k == 2 else pl.ds(8, count - 8)
-                src = dst = dst.at[part]
         else:
             src = g.at[t, core, a3, a2] if stage == 1 else g.at[t, core, a3]
-            if k >= 2:
-                src = src.at[half]
+            if stage == 2 and k >= 2:
+                src = src.at[pl.ds(2 * (k % 2), 2)]
             dst = src
-        n = p * 12 + stage * 4 + k
+        n = p * 10 + stage * 3 + k
         return remote(src, dst, send.at[t, n], recv.at[t, n], device_of(beside(at, dims[stage], delta), core))
 
     def keep(p, t):
@@ -301,42 +297,48 @@
             bias_ref.at[t, pl.ds(first, count), :], gs[p].at[t, core, a3, a2, a1], lsem.at[t, p]
         )
 
-    def share(p, t):
-        half = gs[p].at[t, core]
-        return remote(half, half, psend.at[t, p], precv.at[t, p], partner)
+    def share(p, k, t):
+        a3 = lax.rem(at[ORDERS[p][2]] + (0, 3, 1, 2)[k], 4)
+        plane = gs[p].at[t, core, a3]
+        return remote(plane, plane, psend.at[t, p * 4 + k], precv.at[t, p * 4 + k], partner)
 
     def gather_step(n, t):
         parts = range(3)
         if n == 0:
             for p in parts:
                 keep(p, t).start()
-                for k in (0, 1):
+                for k in range(3):
                     gather_copy(0, p, k, t).start()
-        elif n in (1, 3, 5):
-            stage = n // 2
+        elif n in (1, 2):
+            for p in parts:
+                if n == 1:
+                    keep(p, t).wait()
+                for k in range(3):
+                    gather_copy(n - 1, p, k, t).wait_recv()
+                for k in range(3 if n == 1 else 2):
+                    gather_copy(n, p, k, t).start()
+            if n == 2:
+                for p in parts:
+                    share(p, 0, t).start()
+        elif n == 3:
             for p in parts:
                 for k in (0, 1):
-                    gather_copy(stage, p, k, t).wait_recv()
-                    gather_copy(stage, p, k + 2, t).start()
-        elif n in (2, 4):
-            stage = n // 2
+                    gather_copy(2, p, k, t).wait_recv()
+                    gather_copy(2, p, k + 2, t).start()
             for p in parts:
-                if n == 2:
-                    keep(p, t).wait()
-                for k in (2, 3):
-                    gather_copy(stage - 1, p, k, t).wait_recv()
                 for k in (0, 1):
-                    gather_copy(stage, p, k, t).start()
-        elif n == 6:
+                    share(p, k + 1, t).start()
+        elif n == 4:
             for p in parts:
                 for k in (2, 3):
                     gather_copy(2, p, k, t).wait_recv()
-                share(p, t).start()
+                share(p, 3, t).start()
         else:
             for p in parts:
-                share(p, t).wait()
+                for k in range(4):
+                    share(p, k, t).wait()
                 for stage in range(3):
-                    for k in range(4):
+                    for k in range(3 if stage < 2 else 4):
                         gather_copy(stage, p, k, t).wait_send()
 
     def direct(c, t):
@@ -406,29 +408,26 @@
         def _():
             otherwise()
 
-    def exit_first(t):
-        for zz in range(2):
-            for delta in (1, 2, 3):
-                hop(delta, zz, t).start()
-        for zz in range(2):
-            here, rem, loc = mirror(0, zz, t)
-            either(here, loc.start, rem.start)
+    def exit_first(t, zz):
+        for delta in (1, 2, 3):
+            hop(delta, zz, t).start()
+        here, rem, loc = mirror(0, zz, t)
+        either(here, loc.start, rem.start)
 
         def go(n, _):
-            c = lax.rem(col + n, 8)
+            c = zz * 4 + lax.rem(at["x"] + n, 4)
             either(
                 2 * c + t // 2 == row, lambda: direct_local(c, t).start(), lambda: direct_remote(c, t).start()
             )
             return 0
 
-        lax.fori_loop(0, 8, go, 0)
-
-    def exit_second(t):
+        lax.fori_loop(0, 4, go, 0)
+
+    def exit_second(t, zz):
         for n in (1, 2, 3):
-            for zz in range(2):
-                hop_arrival(n - 1, zz, t).wait_recv()
-                here, rem, loc = mirror(n, zz, t)
-                either(here, loc.start, rem.start)
+            hop_arrival(n - 1, zz, t).wait_recv()
+            here, rem, loc = mirror(n, zz, t)
+            either(here, loc.start, rem.start)
 
     def project(j):
         p = jnp.dot(layer_norm(xs[:, j].reshape(1024, 128)), wa_ref[...], preferred_element_type=F32)
@@ -524,12 +523,13 @@
     own = pltpu.make_async_copy(pair_ref.at[row], xs.at[row], osem)
     own.start()
     gather_step(0, 0)
-    for n in range(1, 8):
-        for d in range(3 * n - 3, min(3 * n, 15)):
+    gather_step(0, 1)
+    for n in range(1, 5):
+        for d in range(4 * n - 4, min(4 * n, 15)):
             a2a(d).start()
         gather_step(n, 0)
-        if n in (2, 4, 6):
-            gather_step(n // 2 - 1, 1)
+        if n < 3:
+            gather_step(n, 1)
     own.wait()
     for n in range(15):
         a2a(n).wait()
@@ -554,11 +554,19 @@
 
             @pl.when(jnp.logical_and(hh == 1, t > 0))
             def _():
-                exit_first(t - 1)
+                exit_first(t - 1, 1)
+
+            @pl.when(jnp.logical_and(hh == 0, t > 0))
+            def _():
+                exit_second(t - 1, 0)
 
             @pl.when(jnp.logical_and(hh == 4, t > 0))
             def _():
-                exit_second(t - 1)
+                exit_second(t - 1, 1)
+
+            @pl.when(hh == 5)
+            def _():
+                exit_first(t, 0)
 
             def two(i, _):
                 task(t * 32 + hh * 4 + i * 2, 0)
@@ -575,8 +583,9 @@
     acc_s[1] = jnp.ones((144, 256), F32)
     lax.fori_loop(0, 4, chunk, 0)
     finish(3, 3, 7, acc_s[1])
-    exit_first(3)
-    exit_second(3)
+    exit_first(3, 1)
+    exit_second(3, 0)
+    exit_second(3, 1)
 
     def drain(t, _):
         def one(c, _):
@@ -638,7 +647,7 @@
             pltpu.VMEM((8, 1024, 128), BF),
             pltpu.VMEM((4, 3, 2, 8, 32, 128), BF),
             dma((15,)), dma((15,)), dma,
-            dma((4, 36)), dma((4, 36)), dma((4, 3)), dma((4, 3)), dma((4, 3)),
+            dma((4, 30)), dma((4, 30)), dma((4, 3)), dma((4, 12)), dma((4, 12)),
             dma((4, 8)), dma((2, 16)), dma((4, 3, 2)), dma((4, 3, 2)), dma((4, 4, 2)), dma((4, 8)), dma((2, 4)),
         ],
         compiler_params=pltpu.CompilerParams(collective_id=1, has_side_effects=True, vmem_limit_bytes=60 << 20),
@@ -691,7 +700,7 @@
     sub = jnp.pad(info.T, ((0, 0), (0, 124)))
     lane = jnp.arange(128, dtype=jnp.int32)[None, :] // 8 == lax.rem(device, 16)
     lane = jnp.where(lane, jnp.tile(info, (2, 16)), 0.0)
-    wd = jnp.pad(w_dist, ((0, 1), (0, 0)))
+    wd = jnp.pad(w_dist, ((0, 89), (0, 0)))
     wb = jnp.pad(w_bias.T, ((0, 4), (0, 0)))
     pair, bias = embed(z_trunk, sub, lane, wd, wb)
     direct, mirror = main(pair, bias, w_attn, w_out)

time: 234 us -> 211 us (0.902)
  Pallas kernels: 221 us -> 198 us
    pallas_call x1, Pallas kernels: 180 us -> 164 us  [main(): pl.pallas_call(main_kernel, out_shape=(jax.ShapeDtypeStruct((16, 8, 64, 1...]
    pallas_call x1, Pallas kernels: 29.7 us -> 23 us  [embed(): pl.pallas_call(embed_kernel, out_shape=(jax.ShapeDtypeStruct((16, 8, 64,...]
where the time goes in v4:
time: 211 us; the launch traced here: 210 us
  Pallas kernels  198 us (94%)
  local copies, waits for them, and re-layouts  11.5 us (5%)
    pallas_call x1, Pallas kernels, main(): pl.pallas_call(main_kernel, out_shape=(jax.ShapeDtypeStruct((16, 8, 64, 1...  164 us
    pallas_call x1, Pallas kernels, embed(): pl.pallas_call(embed_kernel, out_shape=(jax.ShapeDtypeStruct((16, 8, 64,...  23 us
    pallas_call x1, Pallas kernels, logits(): pl.pallas_call(logits_kernel, grid=(8,), out_shape=jax.ShapeDtypeStruct((...  11.3 us
    unnamed x13, local copies, waits for them, and re-layouts  9.12 us

profile of v4, /device:TPU:31, one launch (start us, length us, event | category | flops | bytes accessed | tf_op | source)
XLA Modules:
  0.0 210.2 jit_solution(14960225913703151989)
XLA Ops:
  0.0 0.7 pad.22.wb_ref
  0.7 0.8 copy.15
  1.4 0.7 copy.16
  2.2 0.1 fusion.1
  2.3 0.1 add_convert_fusion
  2.3 0.1 copy.17
  2.4 0.7 pad.21.wd_ref
  3.1 0.8 copy.18
  4.0 0.8 copy.19
  4.8 0.1 pad.24.we_ref
  4.9 0.1 tile.10
  5.0 0.0 copy-start
  5.0 1.6 copy-done
  6.6 23.0 %embed.1 = (bf16[16,8,64,128]{3,2,1,0:T(8,128)(2,1)S(1)}, f32[4,64,128]{2,1,0:T(8,128)S(1)}) custom-call(bf16[64,128,128]{2,1,0:T(8,128)(2,1)S(1)} %copy-done, f32[8,128]{1,0:T(8,128)S(1)} %pad.20.sub_ref, f32[8,128]{1,0:T(8,128)S(1)} %broadcast_select_fusion.lane_ref, bf16[128,128]{1,0:T(8,128)(2,1)S(1)} %pad.21.wd_ref, bf16[8,128]{1,0:T(8,128)(2,1)S(1)} %pad.22.wb_ref), custom_call_target="tpu_custom_call" | custom-call | tf_op jit(solution)/shard_map/embed/pallas_call | solution.py:178
  29.6 0.0 copy-start.1
  29.6 1.3 copy-done.1
  30.9 0.0 copy-start.4
  30.9 0.6 copy-done.4
  31.6 164.1 %main.1 = (bf16[16,8,64,128]{3,2,1,0:T(8,128)(2,1)}, bf16[8,8,128,128]{3,2,1,0:T(8,128)(2,1)}) custom-call(bf16[16,8,64,128]{3,2,1,0:T(8,128)(2,1)} %copy-done.1, f32[4,64,128]{2,1,0:T(8,128)} %copy-done.4, bf16[128,512]{1,0:T(8,128)(2,1)} %wa_ref.1, bf16[128,128]{1,0:T(8,128)(2,1)} %wo_ref.1), custom_call_target="tpu_custom_call" | custom-call | tf_op jit(solution)/shard_map/main/pallas_call | solution.py:632
  195.7 0.0 copy-start.2
  195.7 1.6 copy-done.2
  197.2 0.0 copy-start.3
  197.2 1.6 copy-done.3
  198.8 11.3 %logits.1 = f32[64,128,128]{2,1,0:T(8,128)} custom-call(bf16[16,8,64,128]{3,2,1,0:T(8,128)(2,1)S(1)} %copy-done.2, bf16[64,128,128]{2,1,0:T(8,128)(2,1)S(1)} %bitcast.7, bf16[128,128]{1,0:T(8,128)(2,1)S(1)} %pad.23.wp_ref, bf16[128,128]{1,0:T(8,128)(2,1)S(1)} %pad.24.we_ref), custom_call_target="tpu_custom_call" | custom-call | tf_op jit(solution)/shard_map/logits/pallas_call | solution.py:680
  (5 shorter events, 0.0 us)
Async XLA Ops:
  5.0 1.6 copy-start
  29.6 1.3 copy-start.1
  30.9 0.6 copy-start.4
  195.7 1.6 copy-start.2
  197.2 1.6 copy-start.3

commit v5 on v4

--- a/solution.py
+++ b/solution.py
@@ -17,9 +17,9 @@
     (1, 0, 0), (3, 0, 0), (0, 1, 0), (2, 0, 0), (1, 1, 0), (3, 1, 0), (0, 0, 1), (2, 1, 0),
     (1, 0, 1), (3, 0, 1), (0, 1, 1), (2, 0, 1), (1, 1, 1), (3, 1, 1), (2, 1, 1),
 )
-PREPARE = {0: (1, 3), 1: (2, 0), 5: (0, 5), 7: (2, 1)}
+PREPARE = {0: (1, 3), 1: (2, 0), 3: (0, 5)}
 ATTEND = {
-    (0, 0): (1, 4), (0, 2): (2, 2), (0, 3): (3, 0), (0, 4): (1, 5), (0, 5): (2, 3), (0, 6): (3, 1),
+    (0, 0): (1, 4), (0, 1): (2, 1), (0, 2): (2, 2), (0, 3): (3, 0), (0, 4): (1, 5), (0, 5): (2, 3), (0, 6): (3, 1),
     (1, 0): (2, 4), (1, 1): (3, 2), (1, 3): (2, 5), (1, 4): (3, 3), (1, 7): (3, 4), (2, 2): (3, 5),
 }
 
@@ -38,12 +38,23 @@
     )
 
 
-def embed_kernel(z_ref, sub_ref, lane_ref, wd_ref, wb_ref, pair_ref, bias_ref,
-                 rs, rl, flat, s_send, s_recv, l_send, l_recv):
+def embed_kernel(z_hbm, coords_ref, mask_ref, wd_raw, wb_ref, pair_hbm, bias_ref,
+                 z_ref, pair_s, wd_ref, info, sub_ref, lane_ref, rs, rl, flat,
+                 s_send, s_recv, l_send, l_recv, z_sem, out_sem):
+    load_z = pltpu.make_async_copy(z_hbm, z_ref, z_sem)
+    load_z.start()
     row = lax.axis_index("row")
     col = lax.axis_index("col")
     slot = lax.rem(row, 2) * 8 + col
     target = row // 2
+    info[...] = jnp.zeros((8, 128), F32)
+    info[0:3, 0:8] = coords_ref[...].astype(F32)
+    info[3:4, 0:8] = mask_ref[...].astype(F32)
+    tokens = info[...]
+    sub_ref[...] = jnp.concatenate([tokens] * 16, axis=0).T[0:8]
+    lane_ref[...] = pltpu.roll(tokens, slot * 8, 1)
+    wd_ref[...] = jnp.zeros((128, 128), BF)
+    wd_ref[0:39] = wd_raw[...]
     barrier = pltpu.get_barrier_semaphore()
 
     def greet_row(d, _):
@@ -131,6 +142,8 @@
     lower = jnp.where(edge == 0, -1, jnp.where(edge >= 39, big, lower_edge * lower_edge)).astype(F32)
     upper = jnp.where(edge >= 38, big, upper_edge * upper_edge).astype(F32)
     head = lax.broadcasted_iota(jnp.int32, (8, 128), 1) // 32
+
+    load_z.wait()
 
     def eight(t, _):
         own = rs[t]
@@ -165,36 +178,53 @@
 
     lax.fori_loop(0, 8, eight, 0, unroll=4)
 
+    def out_copy(g):
+        return pltpu.make_async_copy(pair_s.at[g], pair_hbm.at[g], out_sem.at[g])
+
     def out(g, _):
         for j in range(8):
             at = pl.multiple_of((g * 8 + j) * 64, 64)
-            pair_ref[g, j] = flat[pl.ds(at, 64), :].astype(BF)
+            pair_s[g, j] = flat[pl.ds(at, 64), :].astype(BF)
+
+        @pl.when(g > 0)
+        def _():
+            out_copy(g - 1).start()
+
         return 0
 
     lax.fori_loop(0, 16, out, 0)
-
-
-def embed(z, sub, lane, wd, wb):
+    out_copy(15).start()
+    for g in range(16):
+        out_copy(g).wait()
+
+
+def embed(z, coords, mask, wd, wb):
+    any_spec = pl.BlockSpec(memory_space=pl.ANY)
+    vmem = pl.BlockSpec(memory_space=pltpu.VMEM)
+    dma = pltpu.SemaphoreType.DMA
     return pl.pallas_call(
         embed_kernel,
         out_shape=(
             jax.ShapeDtypeStruct((16, 8, 64, 128), BF),
             jax.ShapeDtypeStruct((4, 64, 128), F32),
         ),
-        in_specs=[pl.BlockSpec(memory_space=pltpu.VMEM)] * 5,
-        out_specs=(pl.BlockSpec(memory_space=pltpu.VMEM),) * 2,
+        in_specs=[any_spec, vmem, vmem, vmem, vmem],
+        out_specs=(any_spec, vmem),
         scratch_shapes=[
+            pltpu.VMEM((64, 128, 128), BF),
+            pltpu.VMEM((16, 8, 64, 128), BF),
+            pltpu.VMEM((128, 128), BF),
+            pltpu.VMEM((8, 128), F32),
+            pltpu.VMEM((8, 128), F32),
+            pltpu.VMEM((8, 128), F32),
             pltpu.VMEM((8, 8, 128), F32),
             pltpu.VMEM((16, 8, 128), F32),
             pltpu.VMEM((8192, 128), F32),
-            pltpu.SemaphoreType.DMA((7,)),
-            pltpu.SemaphoreType.DMA((7,)),
-            pltpu.SemaphoreType.DMA((16,)),
-            pltpu.SemaphoreType.DMA((16,)),
+            dma((7,)), dma((7,)), dma((16,)), dma((16,)), dma, dma((16,)),
         ],
-        compiler_params=pltpu.CompilerParams(collective_id=0, has_side_effects=True, vmem_limit_bytes=40 << 20),
+        compiler_params=pltpu.CompilerParams(collective_id=0, has_side_effects=True, vmem_limit_bytes=63 << 20),
         name="embed",
-    )(z, sub, lane, wd, wb)
+    )(z, coords, mask, wd, wb)
 
 
 def place():
@@ -265,10 +295,13 @@
     def _():
         pl.semaphore_wait(barrier, 31)
 
-    def a2a(n):
+    def a2a(n, half):
         dy, dz, dc = SPREAD[n]
         to = lax.rem(at["y"] + dy, 4) * 4 + lax.rem(lax.rem(row // 2, 2) + dz, 2) * 2 + lax.rem(core + dc, 2)
-        return remote(pair_ref.at[to], xs.at[row], asend.at[n], arecv.at[n], (to, col))
+        cols = pl.ds(half * 4, 4)
+        return remote(
+            pair_ref.at[to, cols], xs.at[row, cols], asend.at[half, n], arecv.at[half, n], (to, col)
+        )
 
     def gather_copy(stage, p, k, t):
         dims = ORDERS[p]
@@ -460,7 +493,11 @@
     minor = (((1,), (1,)), ((), ()))
 
     def split(f):
-        return f // 32, lax.rem(f, 32) // 8, lax.rem(f, 8)
+        n = lax.rem(f, 32)
+        first = f < 32
+        cp = jnp.where(first, lax.rem(n, 16) // 4, n // 8)
+        j = jnp.where(first, (n // 16) * 4 + lax.rem(n, 4), lax.rem(n, 8))
+        return f // 32, cp, j
 
     def queries(t, cp, j):
         parts = []
@@ -525,14 +562,14 @@
     gather_step(0, 0)
     gather_step(0, 1)
     for n in range(1, 5):
-        for d in range(4 * n - 4, min(4 * n, 15)):
-            a2a(d).start()
+        for d in range(8 * n - 8, min(8 * n, 30)):
+            a2a(d % 15, d // 15).start()
         gather_step(n, 0)
         if n < 3:
             gather_step(n, 1)
     own.wait()
     for n in range(15):
-        a2a(n).wait()
+        a2a(n, 0).wait()
 
     def prepare(j, _):
         for n, (chunk, step) in PREPARE.items():
@@ -543,7 +580,7 @@
         project(j)
         return 0
 
-    lax.fori_loop(0, 8, prepare, 0)
+    lax.fori_loop(0, 4, prepare, 0)
 
     def chunk(t, _):
         def half(hh, _):
@@ -552,11 +589,26 @@
                 def _():
                     gather_step(step, later)
 
+            @pl.when(jnp.logical_and(hh == 3, t == 0))
+            def _():
+                for n in range(15):
+                    a2a(n, 1).wait()
+
+                def late(j, _):
+                    project(j)
+                    return 0
+
+                lax.fori_loop(4, 8, late, 0)
+
+            @pl.when(jnp.logical_and(hh == 0, t == 1))
+            def _():
+                exit_first(0, 0)
+
             @pl.when(jnp.logical_and(hh == 1, t > 0))
             def _():
                 exit_first(t - 1, 1)
 
-            @pl.when(jnp.logical_and(hh == 0, t > 0))
+            @pl.when(jnp.logical_or(jnp.logical_and(hh == 0, t > 1), jnp.logical_and(hh == 3, t == 1)))
             def _():
                 exit_second(t - 1, 0)
 
@@ -564,7 +616,7 @@
             def _():
                 exit_second(t - 1, 1)
 
-            @pl.when(hh == 5)
+            @pl.when(jnp.logical_and(hh == 5, t > 0))
             def _():
                 exit_first(t, 0)
 
@@ -646,7 +698,7 @@
             pltpu.VMEM((2, 144, 256), F32),
             pltpu.VMEM((8, 1024, 128), BF),
             pltpu.VMEM((4, 3, 2, 8, 32, 128), BF),
-            dma((15,)), dma((15,)), dma,
+            dma((2, 15)), dma((2, 15)), dma,
             dma((4, 30)), dma((4, 30)), dma((4, 3)), dma((4, 12)), dma((4, 12)),
             dma((4, 8)), dma((2, 16)), dma((4, 3, 2)), dma((4, 3, 2)), dma((4, 4, 2)), dma((4, 8)), dma((2, 4)),
         ],
@@ -655,25 +707,21 @@
     )(pair, bias, wa, wo)
 
 
-def logits_kernel(d_ref, m_ref, wp_ref, we_ref, o_ref, flat):
-    step = pl.program_id(0)
-
-    @pl.when(step == 0)
+def logits_kernel(d_ref, m_ref, wp_ref, we_ref, o_ref, flat, wp_s, we_s):
+    @pl.when(pl.program_id(0) == 0)
     def _():
-        def widen(g, _):
-            for j in range(8):
-                at = pl.multiple_of((g * 8 + j) * 64, 64)
-                flat[pl.ds(at, 64), :] = d_ref[g, j].astype(F32)
-            return 0
-
-        lax.fori_loop(0, 16, widen, 0)
-
-    for a in range(8):
-        u = flat[pl.ds(step * 8 + a, 128, stride=64), :]
-        sym = u + m_ref[a].astype(F32)
-        pae = jnp.dot(layer_norm(u), wp_ref[...], preferred_element_type=F32)
-        pde = jnp.dot(layer_norm(sym), we_ref[...], preferred_element_type=F32)
-        o_ref[a] = pae + pde
+        wp_s[...] = jnp.zeros((128, 128), BF)
+        we_s[...] = jnp.zeros((128, 128), BF)
+        wp_s[0:64] = wp_ref[...]
+        we_s[64:128] = we_ref[...]
+
+    flat[...] = d_ref[...].reshape(1024, 128).astype(F32)
+    u = jnp.concatenate([flat[pl.ds(a, 128, stride=8), :] for a in range(8)], axis=0)
+    sym = u + m_ref[...].reshape(1024, 128).astype(F32)
+    minor = (((1,), (1,)), ((), ()))
+    pae = lax.dot_general(layer_norm(u), wp_s[...], minor, preferred_element_type=F32)
+    pde = lax.dot_general(layer_norm(sym), we_s[...], minor, preferred_element_type=F32)
+    o_ref[...] = (pae + pde).reshape(8, 128, 128)
 
 
 def logits(d, m, wp, we):
@@ -682,31 +730,22 @@
         grid=(8,),
         out_shape=jax.ShapeDtypeStruct((64, 128, 128), F32),
         in_specs=[
-            pl.BlockSpec((16, 8, 64, 128), lambda t: (0, 0, 0, 0)),
+            pl.BlockSpec((16, 8, 8, 128), lambda t: (0, 0, t, 0)),
             pl.BlockSpec((8, 128, 128), lambda t: (t, 0, 0)),
-            pl.BlockSpec((128, 128), lambda t: (0, 0)),
-            pl.BlockSpec((128, 128), lambda t: (0, 0)),
+            pl.BlockSpec((64, 128), lambda t: (0, 0)),
+            pl.BlockSpec((64, 128), lambda t: (0, 0)),
         ],
         out_specs=pl.BlockSpec((8, 128, 128), lambda t: (t, 0, 0)),
-        scratch_shapes=[pltpu.VMEM((8192, 128), F32)],
-        compiler_params=pltpu.CompilerParams(vmem_limit_bytes=40 << 20),
+        scratch_shapes=[pltpu.VMEM((1024, 128), F32), pltpu.VMEM((128, 128), BF), pltpu.VMEM((128, 128), BF)],
+        compiler_params=pltpu.CompilerParams(vmem_limit_bytes=63 << 20),
         name="logits",
     )(d, m, wp, we)
 
 
 def per_device(z_trunk, coords, token_mask, w_dist, w_attn, w_bias, w_out, w_pae, w_pde):
-    device = lax.axis_index("row") * 8 + lax.axis_index("col")
-    info = jnp.concatenate([coords, token_mask[None]], axis=0).astype(F32)
-    sub = jnp.pad(info.T, ((0, 0), (0, 124)))
-    lane = jnp.arange(128, dtype=jnp.int32)[None, :] // 8 == lax.rem(device, 16)
-    lane = jnp.where(lane, jnp.tile(info, (2, 16)), 0.0)
-    wd = jnp.pad(w_dist, ((0, 89), (0, 0)))
-    wb = jnp.pad(w_bias.T, ((0, 4), (0, 0)))
-    pair, bias = embed(z_trunk, sub, lane, wd, wb)
+    pair, bias = embed(z_trunk, coords, token_mask[None], w_dist, w_bias.T)
     direct, mirror = main(pair, bias, w_attn, w_out)
-    wp = jnp.pad(w_pae, ((0, 0), (0, 64)))
-    we = jnp.pad(w_pde, ((0, 0), (64, 0)))
-    return logits(direct, mirror.reshape(64, 128, 128), wp, we)
+    return logits(direct, mirror.reshape(64, 128, 128), w_pae.T, w_pde.T)
 
 
 def solution(mesh):

time: 211 us -> 195 us (0.924)
  local copies, waits for them, and re-layouts: 11.5 us -> 0 us
  Pallas kernels: 198 us -> 194 us
    unnamed x13 -> x0, local copies, waits for them, and re-layouts: 9.12 us -> none
    pallas_call x1, Pallas kernels: 164 us -> 158 us  [main(): pl.pallas_call(main_kernel, out_shape=(jax.ShapeDtypeStruct((16, 8, 64, 1...]
    pallas_call x1, Pallas kernels: 23 us -> 26 us  [embed(): pl.pallas_call(embed_kernel, out_shape=(jax.ShapeDtypeStruct((16, 8, 64,...]
where the time goes in v5:
time: 195 us; the launch traced here: 194 us
  Pallas kernels  194 us (99%)
    pallas_call x1, Pallas kernels, main(): pl.pallas_call(main_kernel, out_shape=(jax.ShapeDtypeStruct((16, 8, 64, 1...  158 us
    pallas_call x1, Pallas kernels, embed(): pl.pallas_call(embed_kernel, out_shape=(jax.ShapeDtypeStruct((16, 8, 64,...  26 us
    pallas_call x1, Pallas kernels, logits(): pl.pallas_call(logits_kernel, grid=(8,), out_shape=jax.ShapeDtypeStruct((...  9.85 us

profile of v5, /device:TPU:31, one launch (start us, length us, event | category | flops | bytes accessed | tf_op | source)
XLA Modules:
  0.0 193.6 jit_solution(10533683911337787135)
XLA Ops:
  0.0 26.0 %embed.1 = (bf16[16,8,64,128]{3,2,1,0:T(8,128)(2,1)}, f32[4,64,128]{2,1,0:T(8,128)}) custom-call(bf16[64,128,128]{2,1,0:T(8,128)(2,1)} %z_hbm.1, s32[3,8]{1,0:T(4,128)} %coords_ref.1, s32[1,8]{1,0:T(1,128)} %bitcast.9, bf16[39,128]{1,0:T(8,128)(2,1)} %wd_raw.1, bf16[4,128]{1,0:T(4,128)(2,1)} %bitcast.8), custom_call_target="tpu_custom_call" | custom-call | tf_op jit(solution)/shard_map/embed/pallas_call | solution.py:205
  26.0 157.8 %main.1 = (bf16[16,8,64,128]{3,2,1,0:T(8,128)(2,1)}, bf16[8,8,128,128]{3,2,1,0:T(8,128)(2,1)}) custom-call(bf16[16,8,64,128]{3,2,1,0:T(8,128)(2,1)} %get-tuple-element.9.pair_ref, f32[4,64,128]{2,1,0:T(8,128)} %get-tuple-element.10.bias_ref, bf16[128,512]{1,0:T(8,128)(2,1)} %wa_ref.1, bf16[128,128]{1,0:T(8,128)(2,1)} %wo_ref.1), custom_call_target="tpu_custom_call" | custom-call | tf_op jit(solution)/shard_map/main/pallas_call | solution.py:684
  183.8 9.9 %logits.1 = f32[64,128,128]{2,1,0:T(8,128)} custom-call(bf16[16,8,64,128]{3,2,1,0:T(8,128)(2,1)} %get-tuple-element.11.d_ref, bf16[64,128,128]{2,1,0:T(8,128)(2,1)} %bitcast.5, bf16[64,128]{1,0:T(8,128)(2,1)} %bitcast.6, bf16[64,128]{1,0:T(8,128)(2,1)} %bitcast.7), custom_call_target="tpu_custom_call" | custom-call | tf_op jit(solution)/shard_map/logits/pallas_call | solution.py:728

commit v6 on v5

--- a/solution.py
+++ b/solution.py
@@ -580,7 +580,7 @@
         project(j)
         return 0
 
-    lax.fori_loop(0, 4, prepare, 0)
+    lax.fori_loop(0, 4, prepare, 0, unroll=2)
 
     def chunk(t, _):
         def half(hh, _):
@@ -598,7 +598,7 @@
                     project(j)
                     return 0
 
-                lax.fori_loop(4, 8, late, 0)
+                lax.fori_loop(4, 8, late, 0, unroll=2)
 
             @pl.when(jnp.logical_and(hh == 0, t == 1))
             def _():
@@ -608,11 +608,11 @@
             def _():
                 exit_first(t - 1, 1)
 
-            @pl.when(jnp.logical_or(jnp.logical_and(hh == 0, t > 1), jnp.logical_and(hh == 3, t == 1)))
+            @pl.when(jnp.logical_or(jnp.logical_and(hh == 2, t > 1), jnp.logical_and(hh == 3, t == 1)))
             def _():
                 exit_second(t - 1, 0)
 
-            @pl.when(jnp.logical_and(hh == 4, t > 0))
+            @pl.when(jnp.logical_and(hh == 5, t > 0))
             def _():
                 exit_second(t - 1, 1)
 

time: 195 us -> 194 us (level)
  Pallas kernels: 194 us -> 191 us
    pallas_call x1, Pallas kernels: 158 us -> 155 us  [main(): pl.pallas_call(main_kernel, out_shape=(jax.ShapeDtypeStruct((16, 8, 64, 1...]
where the time goes in v6:
time: 194 us; the launch traced here: 191 us
  Pallas kernels  191 us (98%)
    pallas_call x1, Pallas kernels, main(): pl.pallas_call(main_kernel, out_shape=(jax.ShapeDtypeStruct((16, 8, 64, 1...  155 us
    pallas_call x1, Pallas kernels, embed(): pl.pallas_call(embed_kernel, out_shape=(jax.ShapeDtypeStruct((16, 8, 64,...  26 us
    pallas_call x1, Pallas kernels, logits(): pl.pallas_call(logits_kernel, grid=(8,), out_shape=jax.ShapeDtypeStruct((...  9.86 us

profile of v6, /device:TPU:31, one launch (start us, length us, event | category | flops | bytes accessed | tf_op | source)
XLA Modules:
  0.0 191.3 jit_solution(16507862845944960948)
XLA Ops:
  0.0 26.0 %embed.1 = (bf16[16,8,64,128]{3,2,1,0:T(8,128)(2,1)}, f32[4,64,128]{2,1,0:T(8,128)}) custom-call(bf16[64,128,128]{2,1,0:T(8,128)(2,1)} %z_hbm.1, s32[3,8]{1,0:T(4,128)} %coords_ref.1, s32[1,8]{1,0:T(1,128)} %bitcast.9, bf16[39,128]{1,0:T(8,128)(2,1)} %wd_raw.1, bf16[4,128]{1,0:T(4,128)(2,1)} %bitcast.8), custom_call_target="tpu_custom_call" | custom-call | tf_op jit(solution)/shard_map/embed/pallas_call | solution.py:205
  26.0 155.4 %main.1 = (bf16[16,8,64,128]{3,2,1,0:T(8,128)(2,1)}, bf16[8,8,128,128]{3,2,1,0:T(8,128)(2,1)}) custom-call(bf16[16,8,64,128]{3,2,1,0:T(8,128)(2,1)} %get-tuple-element.9.pair_ref, f32[4,64,128]{2,1,0:T(8,128)} %get-tuple-element.10.bias_ref, bf16[128,512]{1,0:T(8,128)(2,1)} %wa_ref.1, bf16[128,128]{1,0:T(8,128)(2,1)} %wo_ref.1), custom_call_target="tpu_custom_call" | custom-call | tf_op jit(solution)/shard_map/main/pallas_call | solution.py:684
  181.5 9.9 %logits.1 = f32[64,128,128]{2,1,0:T(8,128)} custom-call(bf16[16,8,64,128]{3,2,1,0:T(8,128)(2,1)} %get-tuple-element.11.d_ref, bf16[64,128,128]{2,1,0:T(8,128)(2,1)} %bitcast.5, bf16[64,128]{1,0:T(8,128)(2,1)} %bitcast.6, bf16[64,128]{1,0:T(8,128)(2,1)} %bitcast.7), custom_call_target="tpu_custom_call" | custom-call | tf_op jit(solution)/shard_map/logits/pallas_call | solution.py:728
